TPU v7x, 256 devices: a whole 4x4x8 slice. The times are simulated.
256 devices in a mesh: frame: 64 (over y, x_lo, z), patch: 4 (over x_hi, core).
Axes of the slice: x: 4 (x_hi: 2, x_lo: 2; x = x_hi * 2 + x_lo), y: 4, z: 8, core: 2. Of those that a mesh axis runs over, the one named last changes fastest.
Arguments:
- sky_image: float32 [64, 512, 1024], P('frame', None, 'patch'), may hold values from 0.5 to 1.5
- coefficients: float32 [64, 32, 64], P('frame', 'patch'), may hold values from -0.9 to 0.9
- mode_basis: float32 [64, 20736], replicated, may hold values from -6 to 6
- aperture: int32 [144, 144], replicated, may hold values from 0 to 1, as said below
Outputs:
- mode_gradient: float32 [64, 32, 64], P('frame', 'patch')
- object_spectrum: float32 [32, 2, 20736], P('patch', None, 'frame')
Inputs may be any that keep to these rules, and one draw needn't show every extreme that they name: `aperture`: 0 outside an annulus centred at (72, 72) with outer radius between 28 and 36 pixels and a central obstruction; inside it, each pixel is 1 except for randomly placed dead pixels, which are 0.
All inputs are finite; a program needn't handle non-finite values.
Results may differ from a plain program's by a relative error of at most 0.0003.
Values sent between devices are 32-bit elements; how exact they have to be, the bound alone decides.
A program may use at most 128 MiB of HBM per device.

v0:
```python
import math

import jax
import jax.numpy as jnp
from jax import lax
from jax.sharding import PartitionSpec as P

P_SIZE = 144
RIM = 8


reg_weight = 0.02
highest = lax.Precision.HIGHEST


def padded_2(array, sides, width):
    for axis, dim in sides:
        size, length = (lax.axis_size(axis), array.shape[dim])
        up = [(i, (i + 1) % size) for i in range(size - 1)]
        down = [(j, i) for i, j in up]
        last = lax.slice_in_dim(array, length - width, length, axis=dim)
        initial = lax.slice_in_dim(array, 0, width, axis=dim)
        before = lax.ppermute(last, axis, up)
        after = lax.ppermute(initial, axis, down)
        array = jnp.concatenate([before, array, after], axis=dim)
    return array


def window_table():
    offsets = jnp.arange(P_SIZE, dtype=jnp.float32)
    distance = jnp.minimum(offsets, P_SIZE - 1 - offsets)
    taper_value = 0.3 + 0.7 * jnp.sin(math.pi * (distance + 1.0) / (2.0 * (RIM + 1))) ** 2
    profile = jnp.where(distance < RIM, taper_value, 1.0)
    return profile[:, None] * profile[None, :]


def fourier_tables():
    position = jnp.arange(P_SIZE, dtype=jnp.int32)
    product = position[:, None] * position[None, :] % P_SIZE
    angles = 2.0 * math.pi / P_SIZE * product.astype(jnp.float32)
    return (jnp.cos(angles), jnp.sin(angles))


def left_mult(table, field_stack):
    return jnp.einsum("ab,fpbc->fpac", table, field_stack, precision=highest)


def right_mult(field_stack, table):
    return jnp.einsum("fpab,bc->fpac", field_stack, table, precision=highest)


def transform(real_part, imag_part, tables):
    cosine_table, sine_table = tables
    if imag_part is None:
        left_real = left_mult(cosine_table, real_part)
        left_imag = -left_mult(sine_table, real_part)
    else:
        left_real = left_mult(cosine_table, real_part) + left_mult(sine_table, imag_part)
        left_imag = left_mult(cosine_table, imag_part) - left_mult(sine_table, real_part)
    out_real = right_mult(left_real, cosine_table) + right_mult(left_imag, sine_table)
    out_imag = right_mult(left_imag, cosine_table) - right_mult(left_real, sine_table)
    return (out_real, out_imag)


def body(sky_image, coefficients, mode_basis, aperture):
    frames_here, row_total, column_total = sky_image.shape
    patches_here = coefficients.shape[1]
    tile_side = P_SIZE - 2 * RIM
    tables = fourier_tables()
    window = window_table()
    widened = padded_2(sky_image, (("patch", 2),), RIM)
    padded = jnp.pad(widened, ((0, 0), (RIM, RIM), (0, 0)))
    row_count = row_total // tile_side
    column_count = column_total // tile_side
    blocks = []
    for column_place in range(column_count):
        for row_place in range(row_count):
            blocks.append(
                padded[
                    :,
                    row_place * tile_side : row_place * tile_side + P_SIZE,
                    column_place * tile_side : column_place * tile_side + P_SIZE,
                ]
            )
    patches = jnp.stack(blocks, axis=1)
    data_real, data_imag = transform(window * patches, None, tables)
    data_real = data_real / P_SIZE
    data_imag = data_imag / P_SIZE
    pupil_mask = aperture.astype(jnp.float32)
    pupil_area = jnp.sum(pupil_mask)

    def transfer_map(mode_weights):
        phase_map = jnp.einsum("fpk,kx->fpx", mode_weights, mode_basis, precision=highest).reshape(
            frames_here, patches_here, P_SIZE, P_SIZE
        )
        focal_real, focal_imag = transform(
            pupil_mask * jnp.cos(phase_map), pupil_mask * jnp.sin(phase_map), tables
        )
        intensity = (focal_real**2 + focal_imag**2) / (P_SIZE * P_SIZE * pupil_area)
        return transform(intensity, None, tables)

    (otf_real, otf_imag), pullback = jax.vjp(transfer_map, coefficients)
    numer_real = jnp.sum(otf_real * data_real + otf_imag * data_imag, axis=0)
    numer_imag = jnp.sum(otf_real * data_imag - otf_imag * data_real, axis=0)
    power = jnp.sum(otf_real**2 + otf_imag**2, axis=0)
    spectra = jnp.stack([numer_real, numer_imag, power], axis=1).reshape(
        patches_here, 3, P_SIZE * P_SIZE
    )
    frame_total = frames_here * lax.axis_size("frame")
    damping = reg_weight * frame_total
    share = P_SIZE * P_SIZE // lax.axis_size("frame")
    totals = lax.psum(spectra, "frame")
    denominator = totals[:, 2] + damping
    estimate = totals[:, 0:2] / denominator[:, None]
    own_part = lax.dynamic_slice_in_dim(estimate, lax.axis_index("frame") * share, share, 2)
    object_real = estimate[:, 0].reshape(patches_here, P_SIZE, P_SIZE)[None]
    object_imag = estimate[:, 1].reshape(patches_here, P_SIZE, P_SIZE)[None]
    error_real = data_real - (object_real * otf_real - object_imag * otf_imag)
    error_imag = data_imag - (object_real * otf_imag + object_imag * otf_real)
    scale_factor = 2.0 / (P_SIZE * P_SIZE)
    cotangent_real = -scale_factor * (error_real * object_real + error_imag * object_imag)
    cotangent_imag = scale_factor * (error_real * object_imag - error_imag * object_real)
    gradient = pullback((cotangent_real, cotangent_imag))[0]
    mode_total = lax.psum(jnp.sum(gradient, axis=0), "frame")
    mode_gradient = gradient - mode_total[None] / frame_total
    return (mode_gradient, own_part)


def solution(mesh):
    in_specs = (P("frame", None, "patch"), P("frame", "patch", None), P(), P())
    out_specs = (P("frame", "patch", None), P("patch", None, "frame"))
    return jax.shard_map(body, mesh=mesh, in_specs=in_specs, out_specs=out_specs, check_vma=False)
```

profile of v0, /device:TPU:4, one launch (start us, length us, event | category | flops | bytes accessed | tf_op | source)
XLA Modules:
  0.0 938.4 jit_solution(11270163691090871212)
XLA Ops:
  11.1 5.1 collective-permute-start.1
  18.0 6.6 fusion.345
  41.0 3.2 fusion.86
  44.2 3.2 convolution_add_fusion.8
  47.4 3.2 convolution_subtract_fusion.2
  51.2 3.3 fusion
  54.5 3.4 convolution_bitcast_fusion
  58.0 3.2 fusion.83
  61.2 3.2 fusion.81
  64.4 3.2 convolution_add_fusion.7
  70.7 3.2 convolution_bitcast_fusion.1
  73.9 3.2 fusion.1
  80.3 3.2 fusion.79
  83.5 3.6 fusion.19
  87.1 3.2 fusion.16
  90.3 5.7 multiply_add_fusion.1
  119.0 597.5 %all-reduce.3.cloned.1.call-done = f32[8,3,20736]{2,0,1:T(8,128)} async-done(((f32[8,3,20736]{2,0,1:T(8,128)}), f32[8,3,20736]{2,0,1:T(8,128)}) %all-reduce.3.cloned.1.call-update) | async-done | bytes 1990672 | tf_op jit(solution)/shard_map/psum | solution.py:112
  726.6 3.3 add_multiply_fusion
  736.6 3.4 fusion.58
  740.0 3.2 fusion.12
  748.9 3.6 fusion.22
  760.5 3.2 fusion.6
  765.1 6.1 fusion.347
  771.2 158.1 %psum.15 = f32[8,64]{1,0:T(8,128)S(1)} all-reduce(f32[8,64]{1,0:T(8,128)S(1)} %fusion.347), channel_id=1, replica_groups=mesh['frame'=64,'patch'=4] {'frame'}, use_global_device_ids=true, to_apply=%region_2.3 | all-reduce | flops 512 | bytes 4096 | tf_op jit(solution)/shard_map/psum | solution.py:124
  (89 shorter events, 85.0 us)
Async XLA Ops:
  7.2 10.8 %copy-start = (f32[1,8,64]{2,1,0:T(8,128)S(1)}, f32[1,8,64]{2,1,0:T(8,128)}, u32[]{:S(2)}) copy-start(f32[1,8,64]{2,1,0:T(8,128)} %param.5) | copy-start | bytes 6148
  7.2 10.0 %copy-start.13 = (s32[144,144]{1,0:T(8,128)S(1)}, s32[144,144]{1,0:T(8,128)}, u32[]{:S(2)}) copy-start(s32[144,144]{1,0:T(8,128)} %param.7) | copy-start | bytes 248836
  7.2 709.4 %all-reduce.3.cloned.1.call-start = ((), (), s32[]{:S(2)}) async-start(), calls=%async_computation | async-start | bytes 3981312 | tf_op jit(solution)/shard_map/psum | solution.py:112
  9.2 58.5 %collective-permute-start = (f32[1,512,8]{2,1,0:T(8,128)}, f32[1,512,8]{2,1,0:T(8,128)S(1)}, u32[]{:S(2)}, u32[]{:S(2)}) collective-permute-start(f32[1,512,8]{2,1,0:T(8,128)} %get-tuple-element.13), channel_id=1, source_target_pairs={{0,1},{1,2},{2,3},{4,5},{5,6},{6,7},{8,9},{9,10},{10,11},{12,13},{... | collective-permute-start | bytes 49160 | tf_op jit(solution)/shard_map/ppermute | solution.py:23
  11.1 56.6 %collective-permute-start.1 = (f32[1,512,8]{2,1,0:T(8,128)}, f32[1,512,8]{2,1,0:T(8,128)}, u32[]{:S(2)}, u32[]{:S(2)}) collective-permute-start(f32[1,512,8]{2,1,0:T(8,128)} %get-tuple-element.14), channel_id=1, source_target_pairs={{1,0},{2,1},{3,2},{5,4},{6,5},{7,6},{9,8},{10,9},{11,10},{13,12},{... | collective-permute-start | bytes 49160 | tf_op jit(solution)/shard_map/ppermute | solution.py:24
  18.0 20.9 %copy-start.6 = (f32[144,144]{0,1:T(8,128)}, f32[144,144]{0,1:T(8,128)S(1)}, u32[]{:S(2)}) copy-start(f32[144,144]{0,1:T(8,128)S(1)} %copy.38) | copy-start | bytes 248836
  24.6 0.9 copy-start.9
  24.6 2.3 copy-start.8
  47.4 7.1 copy-start.4
  64.4 3.3 copy-start.2
  90.3 5.7 copy-start.3
  719.1 1.5 copy-start.10
  745.5 1.7 copy-start.5
  755.6 1.7 copy-start.7
  755.6 1.7 copy-start.12
  757.3 3.2 copy-start.11
  765.1 166.3 %copy-start.1 = (f32[1,8,64]{2,1,0:T(8,128)S(1)}, f32[1,8,64]{2,1,0:T(8,128)}, u32[]{:S(2)}) copy-start(f32[1,8,64]{2,1,0:T(8,128)} %param.5) | copy-start | bytes 6148
Sparse Core Ops, SparseCore 0:
  107.2 609.3 all-reduce.2
where the time goes:
time: 949 us; the launch traced here: 938 us
  waiting for transfers between devices  598 us (63%)
  blocking collectives  158 us (17%)
  matrix products  107 us (11%)
  local copies, waits for them, and re-layouts  40.5 us (4%)
  between operations  15.4 us (2%)
  other arithmetic  12.6 us (1%)
    psum x1, waiting for transfers between devices, body(): totals = lax.psum(spectra, 'frame')  598 us
    psum x1, blocking collectives, body(): mode_total = lax.psum(jnp.sum(gradient, axis=0), 'frame')  158 us
    dot_general x20, matrix products, right_mult(): return jnp.einsum('fpab,bc->fpac', field_stack, table, precision=highest)  54.5 us
    dot_general x14, matrix products, left_mult(): return jnp.einsum('ab,fpbc->fpac', table, field_stack, precision=highest)  40 us
  transfers between devices with their start and end apart: 3, of which 1 were waited for; matrix products, arithmetic and copies ran while one was open for 7% of the time, Pallas kernels for 0%

commit v1 on v0

v1 whole, which is shorter than its diff:
```python
import math

import jax
import jax.numpy as jnp
import ml_dtypes
import numpy as np
from jax import lax
from jax.experimental import pallas as pl
from jax.experimental.pallas import tpu as pltpu
from jax.sharding import PartitionSpec as P

SIDE = 144
RIM = 8
TILE = SIDE - 2 * RIM
LOW, BOX = 32, 80
GROUP = 8
DEPTH = 8
STRIPS = 4
FRAMES = GROUP * DEPTH
HALF = SIDE // 2 + 1
CHUNK = SIDE // DEPTH
FLAT = BOX * SIDE
PERIOD = 8 * SIDE
MODES = 64
SHARE = SIDE * SIDE // FRAMES
DAMPING = 0.02 * FRAMES
MESH = pl.DeviceIdType.MESH
f32, bf16 = jnp.float32, jnp.bfloat16


def profile():
    at = np.arange(SIDE, dtype=np.float64)
    distance = np.minimum(at, SIDE - 1 - at)
    taper = 0.3 + 0.7 * np.sin(math.pi * (distance + 1.0) / (2.0 * (RIM + 1))) ** 2
    return np.where(distance < RIM, taper, 1.0)


def tables():
    k = np.arange(SIDE)
    u = np.arange(BOX) + LOW - SIDE // 2
    turn = 2.0 * math.pi / SIDE

    def pair(a, b):
        angle = turn * (np.outer(a, b) % SIDE)
        return np.cos(angle), np.sin(angle)

    parts = {}
    c, s = pair(k, u)
    parts["pupil_left"] = np.concatenate([c, s])
    t = np.zeros((256, 256))
    t[:BOX, :SIDE], t[128 : 128 + BOX, :SIDE] = c.T, s.T
    parts["pupil_right"] = t
    t = np.zeros((SIDE, 256))
    t[:, :BOX], t[:, 128 : 128 + BOX] = c, s
    parts["back_right"] = t
    parts["back_left"] = np.concatenate([c.T, s.T])
    c, s = pair(k, k)
    parts["left"] = np.concatenate([c, s])
    t = np.zeros((SIDE, 256))
    t[:, :HALF], t[:, 128 : 128 + HALF] = c[:, :HALF], -s[:, :HALF]
    parts["right"] = t
    order = np.concatenate([k[RIM:-RIM], k[:RIM], k[-RIM:]])
    t = np.zeros((256, 256))
    w = profile()[:, None]
    t[:SIDE, :HALF], t[:SIDE, 128 : 128 + HALF] = (w * c)[order, :HALF], -(w * s)[order, :HALF]
    parts["data_right"] = t
    t = np.zeros((256, 256))
    twice = np.full((HALF, 1), 2.0)
    twice[0], twice[-1] = 1.0, 1.0
    t[:HALF, :SIDE], t[128 : 128 + HALF, :SIDE] = twice * c[:HALF], -twice * s[:HALF]
    parts["focal_right"] = t
    first, rows = {}, []
    for name, part in parts.items():
        first[name] = (sum(r.shape[0] for r in rows), part.shape[0], part.shape[1])
        rows.append(np.pad(part, ((0, 0), (0, 256 - part.shape[1]))))
    whole = np.concatenate(rows)
    high = whole.astype(ml_dtypes.bfloat16)
    rest = (whole - high.astype(np.float64)).astype(ml_dtypes.bfloat16)
    return np.stack([high, rest]), first


TABLE, FIRST = tables()


def split(x):
    high = x.astype(bf16)
    return high, (x - high.astype(f32)).astype(bf16)


def mm(a, b):
    return jnp.dot(a, b, preferred_element_type=f32)


def mm3(a, b):
    return mm(a[0], b[0]) + (mm(a[0], b[1]) + mm(a[1], b[0]))


def lanes(*parts):
    return jnp.concatenate(parts, axis=1)


def sine_cosine(x):
    quarter = jnp.floor(x * (2.0 / math.pi) + 0.5)
    r = x - quarter * 1.5703125
    r = r - quarter * 4.837512969970703125e-4
    r = r - quarter * 7.54978995489188216e-8
    z = r * r
    sine = ((-1.9515295891e-4 * z + 8.3321608736e-3) * z - 1.6666654611e-1) * z * r + r
    cosine = ((2.443315711809948e-5 * z - 1.388731625493765e-3) * z + 4.166664568298827e-2) * z * z - 0.5 * z + 1.0
    halves = jnp.floor(quarter * 0.5)
    odd = quarter - 2.0 * halves
    minus = 1.0 - 2.0 * (halves - 2.0 * jnp.floor(halves * 0.5))
    swap = odd > 0.5
    return (
        jnp.where(swap, cosine, sine) * minus,
        jnp.where(swap, -sine, cosine) * minus,
    )


def kernel(
    sky, coef, basis, aperture, table_hbm, window_hbm,
    gradient_out, object_out,
    tab, win, skyp, coef_v, coef_send, coef_recv, mask_v, base, base3,
    edges, img, halo, turned, pre, pim, fre, fim, tre, tim, dre, dim_,
    sums, sum_send, sum_recv, sum_v, obj_send, obj_all, ore, oim, dph,
    full, out_send, out_recv, grad_send, grad_recv, ret_send, ret_recv,
    local_sem, coef_ss, coef_rs, img_ss, img_rs, own_ss, own_rs, cross_ss, cross_rs,
    sum_ss, sum_rs, obj_ss, obj_rs, out_ss, out_rs, grad_ss, grad_rs, ret_ss, ret_rs,
):
    place, strip = lax.axis_index("frame"), lax.axis_index("patch")
    me, z = place // DEPTH, place % DEPTH

    def at(group, depth, which=None):
        return {"frame": group * DEPTH + depth, "patch": strip if which is None else which}

    def remote(src, dst, send, recv, device):
        return pltpu.make_async_remote_copy(
            src_ref=src, dst_ref=dst, send_sem=send, recv_sem=recv, device_id=device, device_id_type=MESH
        )

    def table(name):
        row, count, width = FIRST[name]
        return tab[0, row : row + count, :width], tab[1, row : row + count, :width]

    loads = [
        pltpu.make_async_copy(coef.at[0], coef_v, local_sem.at[0]),
        pltpu.make_async_copy(basis.at[:, pl.ds(LOW * SIDE, FLAT)], base, local_sem.at[1]),
        pltpu.make_async_copy(sky.at[0], skyp.at[pl.ds(RIM, 512)], local_sem.at[2]),
        pltpu.make_async_copy(table_hbm, tab, local_sem.at[3]),
        pltpu.make_async_copy(window_hbm, win, local_sem.at[4]),
        pltpu.make_async_copy(aperture, mask_v, local_sem.at[5]),
    ]
    for load in loads:
        load.start()

    barrier = pltpu.get_barrier_semaphore()
    beside = lax.rem(strip + jnp.where(me < 4, STRIPS - 1, 1), STRIPS)

    def greet(device):
        pl.semaphore_signal(barrier, inc=1, device_id=device, device_id_type=MESH)

    for d in range(1, GROUP):
        greet(at(lax.rem(me + d, GROUP), z))
    for d in range(1, DEPTH):
        greet(at(me, lax.rem(z + d, DEPTH)))
    for j in range(GROUP):
        greet(at(j, z, beside))

    skyp[pl.ds(0, RIM), :] = jnp.zeros((RIM, 256), f32)
    skyp[pl.ds(512 + RIM, 120), :] = jnp.zeros((120, 256), f32)
    loads[0].wait()
    for p in range(GROUP):
        row = jnp.broadcast_to(coef_v[p : p + 1, :], (8, MODES))
        coef_send[p * 8 : p * 8 + 8, :] = lanes(row, row)
    loads[2].wait()
    for half in range(2):
        strip_t = skyp[:, half * 128 : half * 128 + 128].T
        edges[2 * half] = strip_t[:8]
        edges[2 * half + 1] = strip_t[120:]
    pl.semaphore_wait(barrier, GROUP - 1 + DEPTH - 1 + GROUP)

    sends = []
    def rows8(ref, j):
        return ref.at[pl.ds(pl.multiple_of(j * 8, 8), 8)]

    for d in range(1, GROUP):
        t = lax.rem(me + d, GROUP)
        c = remote(rows8(coef_send, t), rows8(coef_recv, me), coef_ss.at[t], coef_rs.at[me], at(t, z))
        c.start()
        sends.append(c)
    coef_recv[pl.ds(pl.multiple_of(me * 8, 8), 8), :] = coef_send[pl.ds(pl.multiple_of(me * 8, 8), 8), :]

    def main_of(t):
        return skyp.at[
            pl.ds(pl.multiple_of(lax.rem(t, 4) * TILE, TILE), SIDE), pl.ds(pl.multiple_of((t // 4) * 128, 128), 128)
        ]

    def edge_of(kind, t):
        return edges.at[kind, :, pl.ds(pl.multiple_of(lax.rem(t, 4) * TILE, TILE), 256)]

    for d in range(1, GROUP):
        t = lax.rem(me + d, GROUP)
        c = remote(main_of(t), img.at[me], img_ss.at[t], img_rs.at[me], at(t, z))
        c.start()
        sends.append(c)
        kind, side = jnp.where(t < 4, 2, 1), jnp.where(t < 4, 1, 0)
        c = remote(edge_of(kind, t), halo.at[me, side], own_ss.at[t], own_rs.at[me], at(t, z))
        c.start()
        sends.append(c)
    for p in range(GROUP):
        kind, side, step = (3, 0, 1) if p < 4 else (0, 1, STRIPS - 1)
        c = remote(
            edge_of(kind, p), halo.at[me, side], cross_ss.at[p], cross_rs.at[me],
            at(p, z, lax.rem(strip + step, STRIPS)),
        )
        c.start()
        sends.append(c)
    own_side = jnp.where(me < 4, 1, 0)
    mine = [
        pltpu.make_async_copy(main_of(me), img.at[me], local_sem.at[6]),
        pltpu.make_async_copy(edge_of(jnp.where(me < 4, 2, 1), me), halo.at[me, own_side], local_sem.at[7]),
    ]
    for c in mine:
        c.start()

    loads[1].wait()

    def cut(g, carry):
        at_g = pl.ds(pl.multiple_of(g * PERIOD, 128), PERIOD)
        x = base[:, at_g]
        h, r = split(x)
        base3[0:MODES, at_g] = h
        base3[MODES : 2 * MODES, at_g] = r
        base3[2 * MODES :, at_g] = (x - h.astype(f32) - r.astype(f32)).astype(bf16)
        return carry

    lax.fori_loop(0, BOX // 8, cut, 0)
    for load in loads[3:]:
        load.wait()

    lane = lax.broadcasted_iota(jnp.int32, (8, 128), 1)
    mask = mask_v[LOW : LOW + BOX, 0:128].astype(f32)
    mask = pltpu.roll(mask, 128 - LOW, 1)
    mask = jnp.where(lax.broadcasted_iota(jnp.int32, (BOX, 128), 1) < BOX, mask, 0.0)
    area = jnp.sum(mask)
    intensity_scale = 1.0 / (SIDE * SIDE * area)
    dph[0:BOX, :] = mask

    for d in range(1, GROUP):
        j = lax.rem(me + GROUP - d, GROUP)
        remote(rows8(coef_send, j), rows8(coef_recv, j), coef_ss.at[j], coef_rs.at[j], at(j, z)).wait_recv()
    weights = coef_recv[pl.ds(0, GROUP, stride=8), :]
    w0 = weights.astype(bf16).astype(f32)
    w1 = (weights - w0).astype(bf16).astype(f32)
    w2 = weights - w0 - w1
    weights = jnp.concatenate([lanes(w, w[:, :MODES]) for w in (w0, w1, w2)]).astype(bf16)

    starts = [divmod(SIDE * r + LOW, 128) for r in range(8)]

    def pupils(g, carry):
        ph = mm(weights, base3[:, pl.ds(pl.multiple_of(g * PERIOD, 128), PERIOD)])
        ph = ph[0:8] + (ph[8:16] + ph[16:24])
        rows = []
        for tile, off in starts:
            x = ph[:, tile * 128 : tile * 128 + 128]
            if off:
                x = pltpu.roll(x, 128 - off, 1)
            if off + BOX > 128:
                y = pltpu.roll(ph[:, tile * 128 + 128 : tile * 128 + 256], 128 - off, 1)
                x = jnp.where(lane < 128 - off, x, y)
            rows.append(x)
        m = dph[pl.ds(pl.multiple_of(g * 8, 8), 8), :]
        m = jnp.concatenate([jnp.broadcast_to(m[r : r + 1], (8, 128)) for r in range(8)])
        sine, cosine = sine_cosine(jnp.concatenate(rows))
        at_g = pl.ds(pl.multiple_of(g * 64, 64), 64)
        pre[at_g, :] = m * cosine
        pim[at_g, :] = m * sine
        return carry

    lax.fori_loop(0, BOX // 8, pupils, 0)

    def of_frame(ref, f):
        return ref[pl.ds(f, BOX, stride=GROUP), :]

    def left_forward(x):
        y = mm3(table("left"), split(x))
        return y[:SIDE, :128] + y[SIDE:, 128:], y[:SIDE, 128:] - y[SIDE:, :128]

    def transfers(f, carry):
        b = mm3(table("pupil_left"), split(lanes(of_frame(pre, f), of_frame(pim, f))))
        b_re = b[:SIDE, :128] + b[SIDE:, 128:]
        b_im = b[:SIDE, 128:] - b[SIDE:, :128]
        (rh, rl), (ih, il) = split(b_re), split(b_im)
        field = mm3(
            (
                jnp.concatenate([lanes(rh, ih), lanes(ih, -rh)]),
                jnp.concatenate([lanes(rl, il), lanes(il, -rl)]),
            ),
            table("pupil_right"),
        )
        field_re, field_im = field[:SIDE], field[SIDE:]
        fre[f] = field_re
        fim[f] = field_im
        intensity = (field_re * field_re + field_im * field_im) * intensity_scale
        tre[f], tim[f] = left_forward(mm3(split(intensity[:, :SIDE]), table("right")))
        return carry

    lax.fori_loop(0, GROUP, transfers, 0)

    for c in mine:
        c.wait()
    for j in range(GROUP):
        remote(edge_of(0, 0), halo.at[j, 1 - own_side], cross_ss.at[j], cross_rs.at[j], at(j, z, beside)).wait_recv()
    for d in range(1, GROUP):
        j = lax.rem(me + GROUP - d, GROUP)
        remote(main_of(j), img.at[j], img_ss.at[j], img_rs.at[j], at(j, z)).wait_recv()
        remote(edge_of(0, j), halo.at[j, own_side], own_ss.at[j], own_rs.at[j], at(j, z)).wait_recv()
    row = lax.broadcasted_iota(jnp.int32, (128, 256), 0)
    left_on = jnp.where(jnp.logical_and(strip == 0, me < 4), 0.0, 1.0)
    right_on = jnp.where(jnp.logical_and(strip == STRIPS - 1, me >= 4), 0.0, 1.0)
    rims = halo[...].reshape(128, 256) * jnp.where(lax.rem(row, 16) < 8, left_on, right_on)
    rims = rims.T[:SIDE]
    for f in range(GROUP):
        turned[f] = pltpu.roll(rims, (128 - 16 * f) % 128, 1) if f else rims

    sums[...] = jnp.zeros_like(sums)

    def data(f, carry):
        w = win[...]
        x = lanes(img[f] * w, turned[f] * w)
        d_re, d_im = left_forward(mm3(split(x), table("data_right")))
        dre[f] = d_re
        dim_[f] = d_im
        t_re, t_im = tre[f], tim[f]
        sums[0:SIDE, :] += t_re * d_re + t_im * d_im
        sums[SIDE : 2 * SIDE, :] += t_re * d_im - t_im * d_re
        sums[2 * SIDE :, :] += t_re * t_re + t_im * t_im
        return carry

    lax.fori_loop(0, GROUP, data, 0)

    for d in range(DEPTH):
        for part in range(3):
            sum_send[d, part * CHUNK : part * CHUNK + CHUNK, :] = sums[
                part * SIDE + d * CHUNK : part * SIDE + d * CHUNK + CHUNK, :
            ]
        sum_send[d, 3 * CHUNK :, :] = jnp.zeros((2, 128), f32)
    for d in range(1, DEPTH):
        t = lax.rem(z + d, DEPTH)
        c = remote(sum_send.at[t], sum_recv.at[z], sum_ss.at[t], sum_rs.at[z], at(me, t))
        c.start()
        sends.append(c)
    sum_recv[z] = sum_send[z]
    for d in range(1, DEPTH):
        j = lax.rem(z + DEPTH - d, DEPTH)
        remote(sum_send.at[j], sum_recv.at[j], sum_ss.at[j], sum_rs.at[j], at(me, j)).wait_recv()
    total = sum_recv[0]
    for j in range(1, DEPTH):
        total = total + sum_recv[j]
    sum_v[...] = total
    power = sum_v[2 * CHUNK : 3 * CHUNK, :] + DAMPING
    obj_send[0:CHUNK, :] = sum_v[0:CHUNK, :] / power
    obj_send[CHUNK : 2 * CHUNK, :] = sum_v[CHUNK : 2 * CHUNK, :] / power
    obj_send[2 * CHUNK :, :] = jnp.zeros((4, 128), f32)
    for d in range(1, DEPTH):
        t = lax.rem(z + d, DEPTH)
        c = remote(obj_send, obj_all.at[z], obj_ss.at[t], obj_rs.at[z], at(me, t))
        c.start()
        sends.append(c)
    obj_all[z] = obj_send[...]
    for d in range(1, DEPTH):
        j = lax.rem(z + DEPTH - d, DEPTH)
        remote(obj_send, obj_all.at[j], obj_ss.at[j], obj_rs.at[j], at(me, j)).wait_recv()
    for d in range(DEPTH):
        ore[d * CHUNK : d * CHUNK + CHUNK, :] = obj_all[d, 0:CHUNK, :]
        oim[d * CHUNK : d * CHUNK + CHUNK, :] = obj_all[d, CHUNK : 2 * CHUNK, :]

    r_at = lax.broadcasted_iota(jnp.int32, (SIDE, SIDE), 0)
    c_at = lax.broadcasted_iota(jnp.int32, (SIDE, SIDE), 1)
    flip_rows = jnp.where(lax.rem(r_at + c_at, SIDE) == 0, 1.0, 0.0).astype(bf16)
    r_at = lax.broadcasted_iota(jnp.int32, (128, 256), 0)
    c_at = lax.broadcasted_iota(jnp.int32, (128, 256), 1)
    flip_columns = jnp.where(
        jnp.logical_and(r_at + c_at == SIDE, jnp.logical_and(c_at >= HALF, c_at < SIDE)), 1.0, 0.0
    ).astype(bf16)
    parts = split(lanes(ore[...], oim[...]))
    parts = [mm(flip_rows, part).astype(bf16) for part in parts]
    lane_full = lax.broadcasted_iota(jnp.int32, (SIDE, 128), 1)
    for n, sign in ((0, 1.0), (1, -1.0)):
        mirror = mm(parts[0][:, n * 128 : n * 128 + 128], flip_columns)
        mirror = sign * (mirror + mm(parts[1][:, n * 128 : n * 128 + 128], flip_columns))
        half = (ore, oim)[n][...]
        full[2 * n] = jnp.where(lane_full < HALF, half, mirror[:, :128])
        full[2 * n + 1] = mirror[:, 128:]
    first_row = z * 9 // 4
    for n in range(2):
        placed = [jnp.zeros((8, 128), f32) for _ in range(6)]
        for t in range(3):
            for piece in range(2):
                x = full[2 * n + piece, pl.ds(first_row + t, GROUP, stride=CHUNK), :]
                tile, off = divmod(SIDE * t + 128 * piece, 128)
                if off:
                    x = pltpu.roll(x, off, 1)
                    placed[tile + 1] += jnp.where(lane < off, x, 0.0)
                    x = jnp.where(lane < off, 0.0, x)
                placed[tile] += x
        placed = lanes(*placed)
        picked = jnp.zeros((8, 384), f32)
        for m in range(4):
            moved = pltpu.roll(placed, 768 - 36 * m, 1) if m else placed
            picked = picked + jnp.where(lax.rem(z, 4) == m, 1.0, 0.0) * moved[:, :384]
        for i in range(GROUP):
            out_send[i, n : n + 1, :] = picked[i : i + 1]
    for d in range(1, GROUP):
        t = lax.rem(me + d, GROUP)
        c = remote(out_send.at[t], out_recv.at[me], out_ss.at[t], out_rs.at[me], at(t, z))
        c.start()
        sends.append(c)
    out_recv[me] = out_send[me]

    scale = 2.0 / (SIDE * SIDE)

    def back(f, carry):
        o_re, o_im, t_re, t_im = ore[...], oim[...], tre[f], tim[f]
        e_re = dre[f] - (o_re * t_re - o_im * t_im)
        e_im = dim_[f] - (o_re * t_im + o_im * t_re)
        g_re = -scale * (e_re * o_re + e_im * o_im)
        g_im = scale * (e_re * o_im - e_im * o_re)
        y = mm3(table("left"), split(lanes(g_re, g_im)))
        h = lanes(y[:SIDE, :128] - y[SIDE:, 128:], y[:SIDE, 128:] + y[SIDE:, :128])
        focal = mm3(split(h), table("focal_right")) * (2.0 * intensity_scale)
        g = jnp.concatenate([focal * fre[f], focal * fim[f]])
        y = mm3(split(g[:, :SIDE]), table("back_right"))
        q = lanes(y[:SIDE, :128] - y[SIDE:, 128:], y[:SIDE, 128:] + y[SIDE:, :128])
        y = mm3(table("back_left"), split(q))
        g_re, g_im = y[:BOX, :128] - y[BOX:, 128:], y[:BOX, 128:] + y[BOX:, :128]
        dph[pl.ds(f, BOX, stride=GROUP), :] = of_frame(pre, f) * g_im - of_frame(pim, f) * g_re
        return carry

    lax.fori_loop(0, GROUP, back, 0)

    def project(g, total):
        tiles = [jnp.zeros((8, 128), f32) for _ in range(9)]
        for r, (tile, off) in enumerate(starts):
            x = dph[pl.ds(pl.multiple_of(g * 64, 64) + 8 * r, 8), :]
            if off:
                x = pltpu.roll(x, off, 1)
            if off + BOX > 128:
                tiles[tile + 1] += jnp.where(lane < off, x, 0.0)
                x = jnp.where(lane < off, 0.0, x)
            tiles[tile] += x
        x = jnp.concatenate(split(lanes(*tiles)))
        modes = base3[0 : 2 * MODES, pl.ds(pl.multiple_of(g * PERIOD, 128), PERIOD)]
        return total + lax.dot_general(x, modes, (((1,), (1,)), ((), ())), preferred_element_type=f32)

    total = lax.fori_loop(0, BOX // 8, project, jnp.zeros((16, 128), f32))
    total = total[:8] + total[8:]
    gradient = total + pltpu.roll(total, MODES, 1)

    grad_send[...] = gradient
    for d in range(1, DEPTH):
        t = lax.rem(z + d, DEPTH)
        c = remote(grad_send, grad_recv.at[z], grad_ss.at[t], grad_rs.at[z], at(me, t))
        c.start()
        sends.append(c)
    grad_recv[z] = gradient
    for d in range(1, DEPTH):
        j = lax.rem(z + DEPTH - d, DEPTH)
        remote(grad_send, grad_recv.at[j], grad_ss.at[j], grad_rs.at[j], at(me, j)).wait_recv()
    mean = jnp.sum(grad_recv[...].reshape(64, 128), axis=0, keepdims=True) * (1.0 / FRAMES)
    gradient = gradient - mean
    for j in range(GROUP):
        ret_send[8 * j : 8 * j + 8, :] = jnp.broadcast_to(gradient[j : j + 1], (8, 128))
    for d in range(1, GROUP):
        t = lax.rem(me + d, GROUP)
        c = remote(rows8(ret_send, t), rows8(ret_recv, me), ret_ss.at[t], ret_rs.at[me], at(t, z))
        c.start()
        sends.append(c)
    ret_recv[pl.ds(pl.multiple_of(me * 8, 8), 8), :] = ret_send[pl.ds(pl.multiple_of(me * 8, 8), 8), :]

    for d in range(1, GROUP):
        j = lax.rem(me + GROUP - d, GROUP)
        remote(out_send.at[j], out_recv.at[j], out_ss.at[j], out_rs.at[j], at(j, z)).wait_recv()
    for p in range(GROUP):
        object_out[p] = out_recv[p, 0:2, :SHARE]
    for d in range(1, GROUP):
        j = lax.rem(me + GROUP - d, GROUP)
        remote(rows8(ret_send, j), rows8(ret_recv, j), ret_ss.at[j], ret_rs.at[j], at(j, z)).wait_recv()
    gradient_out[0] = ret_recv[pl.ds(0, GROUP, stride=8), :][:, :MODES]
    for c in sends:
        c.wait_send()


def body(sky_image, coefficients, mode_basis, aperture):
    window = np.broadcast_to((profile() / SIDE).astype(np.float32)[:, None], (SIDE, 128))
    vmem, dma = pltpu.VMEM, pltpu.SemaphoreType.DMA
    scratch = [
        vmem(TABLE.shape, bf16), vmem((SIDE, 128), f32), vmem((640, 256), f32), vmem((GROUP, MODES), f32),
        vmem((64, 128), f32), vmem((64, 128), f32), vmem((SIDE, SIDE), jnp.int32), vmem((MODES, FLAT), f32),
        vmem((3 * MODES, FLAT), bf16),
        vmem((4, 8, 640), f32), vmem((GROUP, SIDE, 128), f32), vmem((GROUP, 2, 8, 256), f32),
        vmem((GROUP, SIDE, 128), f32), vmem((8 * BOX, 128), f32), vmem((8 * BOX, 128), f32),
        vmem((GROUP, SIDE, 256), f32), vmem((GROUP, SIDE, 256), f32),
        *[vmem((GROUP, SIDE, 128), f32)] * 4,
        vmem((3 * SIDE, 128), f32), vmem((DEPTH, 56, 128), f32), vmem((DEPTH, 56, 128), f32), vmem((56, 128), f32),
        vmem((40, 128), f32), vmem((DEPTH, 40, 128), f32), vmem((SIDE, 128), f32), vmem((SIDE, 128), f32),
        vmem((8 * BOX, 128), f32), vmem((4, SIDE, 128), f32), vmem((GROUP, 8, 384), f32), vmem((GROUP, 8, 384), f32),
        vmem((8, 128), f32), vmem((DEPTH, 8, 128), f32), vmem((64, 128), f32), vmem((64, 128), f32),
        *[dma((8,))] * 19,
    ]
    return pl.pallas_call(
        kernel,
        out_shape=(
            jax.ShapeDtypeStruct((1, GROUP, MODES), f32),
            jax.ShapeDtypeStruct((GROUP, 2, SHARE), f32),
        ),
        in_specs=[pl.BlockSpec(memory_space=pl.ANY)] * 6,
        out_specs=[pl.BlockSpec(memory_space=pltpu.VMEM)] * 2,
        scratch_shapes=scratch,
        compiler_params=pltpu.CompilerParams(collective_id=0, has_side_effects=True, vmem_limit_bytes=60 * 2**20),
    )(sky_image, coefficients, mode_basis, aperture, jnp.asarray(TABLE), jnp.asarray(window))


def solution(mesh):
    in_specs = (P("frame", None, "patch"), P("frame", "patch", None), P(), P())
    out_specs = (P("frame", "patch", None), P("patch", None, "frame"))
    return jax.shard_map(body, mesh=mesh, in_specs=in_specs, out_specs=out_specs, check_vma=False)
```

time: 949 us -> 74.3 us (0.08); the launches traced: 938 us -> 73.8 us
  waiting for transfers between devices: 598 us -> 0 us
  blocking collectives: 158 us -> 0 us
  matrix products: 107 us -> 0 us
  Pallas kernels: 0 us -> 69.2 us
  local copies, waits for them, and re-layouts: 40.5 us -> 4 us
  between operations: 15.4 us -> 0.64 us
  other arithmetic: 12.6 us -> 0 us
    psum x1 -> x0, waiting for transfers between devices: 598 us -> none  [body(): totals = lax.psum(spectra, 'frame')]
    psum x1 -> x0, blocking collectives: 158 us -> none  [body(): mode_total = lax.psum(jnp.sum(gradient, axis=0), 'frame')]
    dot_general x36 -> x0, matrix products: 107 us -> none  [the longest x20 54.5 us: right_mult(): return jnp.einsum('fpab,bc->fpac', field_stack, table, precision=highest)]
    pallas_call x0 -> x1, Pallas kernels: none -> 69.2 us  [body(): pl.pallas_call(kernel, out_shape=(jax.ShapeDtypeStruct((1, GROUP, MODES),...]
    another operation x7 -> x1, local copies, waits for them, and re-layouts: 14.8 us -> 1.38 us  [the longest x3 8.09 us: body(): jnp.stack([numer_real, numer_imag, power], axis=1)]
    sin x4 -> x0, local copies, waits for them, and re-layouts: 9.77 us -> none  [transfer_map(): jnp.sin(phase_map)]
  transfers between devices with their start and end apart: 3 -> 0, of which waited for: 1 -> 0; matrix products, arithmetic and copies ran while one was open for 7% -> 0% of each run, Pallas kernels for 0% -> 0%
where the time goes in v1:
time: 74.3 us; the launch traced here: 73.8 us
  Pallas kernels  69.2 us (93%)
  local copies, waits for them, and re-layouts  4 us (5%)
    pallas_call x1, Pallas kernels, body(): pl.pallas_call(kernel, out_shape=(jax.ShapeDtypeStruct((1, GROUP, MODES),...  69.2 us
    unnamed x2, local copies, waits for them, and re-layouts  2.61 us

profile of v1, /device:TPU:4, one launch (start us, length us, event | category | flops | bytes accessed | tf_op | source)
XLA Modules:
  0.0 73.8 jit_solution(1463402429937432835)
XLA Ops:
  0.6 1.4 %jit_solution_.3.window_hbm = f32[144,128]{1,0:T(8,128)} broadcast(f32[144]{0:T(256)} %constant.5.clone), dimensions={0} | broadcast | bytes 74304 | tf_op jit(solution)
  2.0 69.2 %shard_map.77 = (f32[1,8,64]{2,1,0:T(8,128)}, f32[8,2,324]{2,1,0:T(2,128)}) custom-call(f32[1,512,256]{2,1,0:T(8,128)} %sky.1, f32[1,8,64]{2,1,0:T(8,128)} %coef.1, f32[64,20736]{1,0:T(8,128)} %basis.1, s32[144,144]{1,0:T(8,128)} %aperture.1, bf16[2,1792,256]{2,1,0:T(8,128)(2,1)} %constant.4.clone.table_hbm, f32[144,128]{1,0:T(8,128)} %jit_solution_.3.window_hbm), custom_call_target="tpu_custom_call" | custom-call | tf_op jit(solution)/shard_map/pallas_call | solution.py:511
  71.2 1.3 %copy.10 = f32[1,8,64]{2,1,0:T(8,128)} copy(f32[1,8,64]{2,1,0:T(8,128)} %get-tuple-element.4) | data formatting | bytes 4096
  72.5 1.4 %copy.11 = f32[8,2,324]{2,1,0:T(2,128)} copy(f32[8,2,324]{2,1,0:T(2,128)} %get-tuple-element.5) | data formatting | bytes 41472

commit v2 on v1

--- a/solution.py
+++ b/solution.py
@@ -18,10 +18,16 @@
 STRIPS = 4
 FRAMES = GROUP * DEPTH
 HALF = SIDE // 2 + 1
-CHUNK = SIDE // DEPTH
+CHUNK = BOX // DEPTH
+MAIN, REST = 64, HALF - 64
+REST_ROWS = 40
+REST_CHUNK = REST_ROWS // DEPTH
+SUMS = 3 * CHUNK + REST_CHUNK
+OBJECTS = 2 * CHUNK + REST_CHUNK
 FLAT = BOX * SIDE
 PERIOD = 8 * SIDE
 MODES = 64
+UNROLL = 2
 SHARE = SIDE * SIDE // FRAMES
 DAMPING = 0.02 * FRAMES
 MESH = pl.DeviceIdType.MESH
@@ -36,43 +42,45 @@
 
 
 def tables():
-    k = np.arange(SIDE)
+    k = np.arange(HALF)
+    y = np.arange(SIDE)
     u = np.arange(BOX) + LOW - SIDE // 2
-    turn = 2.0 * math.pi / SIDE
+    weight = np.ones(HALF)
+    weight[0] = weight[-1] = 0.5
 
     def pair(a, b):
-        angle = turn * (np.outer(a, b) % SIDE)
+        angle = 2.0 * math.pi / SIDE * (np.outer(a, b) % SIDE)
         return np.cos(angle), np.sin(angle)
+
+    def beside(c, s):
+        t = np.zeros((-(-c.shape[0] // 16) * 16, 256))
+        t[: c.shape[0], : c.shape[1]], t[: c.shape[0], 128 : 128 + c.shape[1]] = c, s
+        return t
+
+    def below(c, s):
+        t = np.zeros((2 * BOX, 256))
+        t[:HALF, : c.shape[1]], t[BOX : BOX + HALF, : c.shape[1]] = c, s
+        return t
 
     parts = {}
     c, s = pair(k, u)
-    parts["pupil_left"] = np.concatenate([c, s])
-    t = np.zeros((256, 256))
-    t[:BOX, :SIDE], t[128 : 128 + BOX, :SIDE] = c.T, s.T
-    parts["pupil_right"] = t
-    t = np.zeros((SIDE, 256))
-    t[:, :BOX], t[:, 128 : 128 + BOX] = c, s
-    parts["back_right"] = t
-    parts["back_left"] = np.concatenate([c.T, s.T])
+    parts["pupil_rows"] = below(c, s)
+    parts["pupil_columns"] = beside(c.T, s.T)
+    parts["back_columns"] = beside(weight[:, None] * c, weight[:, None] * s)
+    parts["back_rows"] = beside(c.T * weight, s.T * weight)
     c, s = pair(k, k)
-    parts["left"] = np.concatenate([c, s])
-    t = np.zeros((SIDE, 256))
-    t[:, :HALF], t[:, 128 : 128 + HALF] = c[:, :HALF], -s[:, :HALF]
-    parts["right"] = t
-    order = np.concatenate([k[RIM:-RIM], k[:RIM], k[-RIM:]])
-    t = np.zeros((256, 256))
-    w = profile()[:, None]
-    t[:SIDE, :HALF], t[:SIDE, 128 : 128 + HALF] = (w * c)[order, :HALF], -(w * s)[order, :HALF]
-    parts["data_right"] = t
-    t = np.zeros((256, 256))
-    twice = np.full((HALF, 1), 2.0)
-    twice[0], twice[-1] = 1.0, 1.0
-    t[:HALF, :SIDE], t[128 : 128 + HALF, :SIDE] = twice * c[:HALF], -twice * s[:HALF]
-    parts["focal_right"] = t
-    first, rows = {}, []
+    parts["focal_columns"] = beside(weight[:, None] * c, -weight[:, None] * s)
+    parts["focal_rows"] = beside(c * weight, s * weight)
+    w = profile()
+    c, s = pair(k, y)
+    parts["data_rows"] = below(c * w / SIDE, s * w / SIDE)
+    order = np.concatenate([y[RIM:-RIM], y[:RIM], y[-RIM:]])
+    parts["data_columns"] = beside((w[:, None] * c.T)[order], -(w[:, None] * s.T)[order])
+    first, rows, total = {}, [], 0
     for name, part in parts.items():
-        first[name] = (sum(r.shape[0] for r in rows), part.shape[0], part.shape[1])
-        rows.append(np.pad(part, ((0, 0), (0, 256 - part.shape[1]))))
+        first[name] = (total, part.shape[0])
+        total += part.shape[0]
+        rows.append(part)
     whole = np.concatenate(rows)
     high = whole.astype(ml_dtypes.bfloat16)
     rest = (whole - high.astype(np.float64)).astype(ml_dtypes.bfloat16)
@@ -118,11 +126,11 @@
 
 
 def kernel(
-    sky, coef, basis, aperture, table_hbm, window_hbm,
+    sky, coef, basis, aperture, table_hbm,
     gradient_out, object_out,
-    tab, win, skyp, coef_v, coef_send, coef_recv, mask_v, base, base3,
-    edges, img, halo, turned, pre, pim, fre, fim, tre, tim, dre, dim_,
-    sums, sum_send, sum_recv, sum_v, obj_send, obj_all, ore, oim, dph,
+    tab, skyp, coef_v, coef_send, coef_recv, mask_v, base, base3,
+    edges, img, halo, turned, pre, pim, fpr, fpi, fmr, fmi, tre, tim, dre, dim_,
+    sums, packed, sum_send, sum_recv, sum_v, obj_send, obj_all, ore, oim, dph,
     full, out_send, out_recv, grad_send, grad_recv, ret_send, ret_recv,
     local_sem, coef_ss, coef_rs, img_ss, img_rs, own_ss, own_rs, cross_ss, cross_rs,
     sum_ss, sum_rs, obj_ss, obj_rs, out_ss, out_rs, grad_ss, grad_rs, ret_ss, ret_rs,
@@ -138,17 +146,16 @@
             src_ref=src, dst_ref=dst, send_sem=send, recv_sem=recv, device_id=device, device_id_type=MESH
         )
 
-    def table(name):
-        row, count, width = FIRST[name]
-        return tab[0, row : row + count, :width], tab[1, row : row + count, :width]
+    def table(name, start, width):
+        row, count = FIRST[name]
+        return tuple(tab[n, row : row + count, start : start + width] for n in range(2))
 
     loads = [
         pltpu.make_async_copy(coef.at[0], coef_v, local_sem.at[0]),
         pltpu.make_async_copy(basis.at[:, pl.ds(LOW * SIDE, FLAT)], base, local_sem.at[1]),
         pltpu.make_async_copy(sky.at[0], skyp.at[pl.ds(RIM, 512)], local_sem.at[2]),
         pltpu.make_async_copy(table_hbm, tab, local_sem.at[3]),
-        pltpu.make_async_copy(window_hbm, win, local_sem.at[4]),
-        pltpu.make_async_copy(aperture, mask_v, local_sem.at[5]),
+        pltpu.make_async_copy(aperture, mask_v, local_sem.at[4]),
     ]
     for load in loads:
         load.start()
@@ -282,30 +289,46 @@
     def of_frame(ref, f):
         return ref[pl.ds(f, BOX, stride=GROUP), :]
 
-    def left_forward(x):
-        y = mm3(table("left"), split(x))
-        return y[:SIDE, :128] + y[SIDE:, 128:], y[:SIDE, 128:] - y[SIDE:, :128]
-
-    def transfers(f, carry):
-        b = mm3(table("pupil_left"), split(lanes(of_frame(pre, f), of_frame(pim, f))))
-        b_re = b[:SIDE, :128] + b[SIDE:, 128:]
-        b_im = b[:SIDE, 128:] - b[SIDE:, :128]
-        (rh, rl), (ih, il) = split(b_re), split(b_im)
-        field = mm3(
-            (
-                jnp.concatenate([lanes(rh, ih), lanes(ih, -rh)]),
-                jnp.concatenate([lanes(rl, il), lanes(il, -rl)]),
-            ),
-            table("pupil_right"),
-        )
-        field_re, field_im = field[:SIDE], field[SIDE:]
-        fre[f] = field_re
-        fim[f] = field_im
-        intensity = (field_re * field_re + field_im * field_im) * intensity_scale
-        tre[f], tim[f] = left_forward(mm3(split(intensity[:, :SIDE]), table("right")))
+    def fold(x):
+        return x[:BOX] + x[BOX:], x[:BOX] - x[BOX:]
+
+    def both(x):
+        h, r = split(x)
+        return h[:, :BOX], r[:, :BOX]
+
+    def stack(*parts):
+        return jnp.concatenate(parts)
+
+    def transfers(n, carry):
+        fs = [n * UNROLL + m for m in range(UNROLL)]
+        rows = []
+        for f in fs:
+            y = mm3(table("pupil_rows", 0, BOX), split(lanes(of_frame(pre, f), of_frame(pim, f))))
+            cr, ci, sr, si = y[:BOX, :128], y[:BOX, 128:], y[BOX:, :128], y[BOX:, 128:]
+            rows += [cr + si, cr - si, ci - sr, ci + sr]
+        y = mm3(both(stack(*rows)), table("pupil_columns", 0, 256))
+        even, odd = [], []
+        for m, f in enumerate(fs):
+            r, i = y[4 * m * BOX : (4 * m + 2) * BOX], y[(4 * m + 2) * BOX : (4 * m + 4) * BOX]
+            p_re, p_im = r[:, :128] + i[:, 128:], i[:, :128] - r[:, 128:]
+            m_re, m_im = r[:, :128] - i[:, 128:], i[:, :128] + r[:, 128:]
+            fpr[f], fpi[f], fmr[f], fmi[f] = p_re, p_im, m_re, m_im
+            plus = (p_re * p_re + p_im * p_im) * intensity_scale
+            minus = (m_re * m_re + m_im * m_im) * intensity_scale
+            even += fold(plus + minus)
+            odd += fold(plus - minus)
+        x_re = mm3(both(stack(*even)), table("focal_columns", 0, 128))
+        x_im = mm3(both(stack(*odd)), table("focal_columns", 128, 128))
+        for m, f in enumerate(fs):
+            x = lanes(x_re[2 * m * BOX : 2 * (m + 1) * BOX], x_im[2 * m * BOX : 2 * (m + 1) * BOX])
+            c = mm3(table("focal_rows", 0, BOX), split(x[:BOX]))
+            s = mm3(table("focal_rows", 128, BOX), split(x[BOX:]))
+            cr, ci, sr, si = c[:, :128], c[:, 128:], s[:, :128], s[:, 128:]
+            tre[f] = stack(cr + si, cr - si)
+            tim[f] = stack(ci - sr, ci + sr)
         return carry
 
-    lax.fori_loop(0, GROUP, transfers, 0)
+    lax.fori_loop(0, GROUP // UNROLL, transfers, 0)
 
     for c in mine:
         c.wait()
@@ -325,26 +348,43 @@
 
     sums[...] = jnp.zeros_like(sums)
 
-    def data(f, carry):
-        w = win[...]
-        x = lanes(img[f] * w, turned[f] * w)
-        d_re, d_im = left_forward(mm3(split(x), table("data_right")))
-        dre[f] = d_re
-        dim_[f] = d_im
-        t_re, t_im = tre[f], tim[f]
-        sums[0:SIDE, :] += t_re * d_re + t_im * d_im
-        sums[SIDE : 2 * SIDE, :] += t_re * d_im - t_im * d_re
-        sums[2 * SIDE :, :] += t_re * t_re + t_im * t_im
+    def data(n, carry):
+        fs = [n * UNROLL + m for m in range(UNROLL)]
+        h, r = split(stack(*[lanes(img[f], turned[f]) for f in fs]))
+        x = mm3((h[:, :SIDE], r[:, :SIDE]), table("data_columns", 0, 256))
+        n_re, n_im, power = sums[0], sums[1], sums[2]
+        for m, f in enumerate(fs):
+            y = mm3(table("data_rows", 0, SIDE), split(x[m * SIDE : (m + 1) * SIDE]))
+            cr, ci, sr, si = y[:BOX, :128], y[:BOX, 128:], y[BOX:, :128], y[BOX:, 128:]
+            d_re, d_im = stack(cr + si, cr - si), stack(ci - sr, ci + sr)
+            dre[f] = d_re
+            dim_[f] = d_im
+            t_re, t_im = tre[f], tim[f]
+            n_re = n_re + (t_re * d_re + t_im * d_im)
+            n_im = n_im + (t_re * d_im - t_im * d_re)
+            power = power + (t_re * t_re + t_im * t_im)
+        sums[0], sums[1], sums[2] = n_re, n_im, power
         return carry
 
-    lax.fori_loop(0, GROUP, data, 0)
-
+    lax.fori_loop(0, GROUP // UNROLL, data, 0)
+
+    lane80 = lax.broadcasted_iota(jnp.int32, (BOX, 128), 1)
+    lane40 = lax.broadcasted_iota(jnp.int32, (REST_ROWS, 128), 1)
+    rest = jnp.zeros((REST_ROWS, 128), f32)
+    for part in range(3):
+        plus, minus = sums[part, :BOX], sums[part, BOX:]
+        packed[part * BOX : (part + 1) * BOX, :] = jnp.where(lane80 < MAIN, plus, pltpu.roll(minus, MAIN, 1))
+        for sign, x in enumerate((plus, minus)):
+            j = (2 * part + sign) * REST
+            x = pltpu.roll(x[:REST_ROWS], (j - MAIN) % 128, 1)
+            rest = jnp.where(jnp.logical_and(lane40 >= j, lane40 < j + REST), x, rest)
+    packed[3 * BOX :, :] = rest
     for d in range(DEPTH):
         for part in range(3):
-            sum_send[d, part * CHUNK : part * CHUNK + CHUNK, :] = sums[
-                part * SIDE + d * CHUNK : part * SIDE + d * CHUNK + CHUNK, :
+            sum_send[d, part * CHUNK : (part + 1) * CHUNK, :] = packed[
+                part * BOX + d * CHUNK : part * BOX + (d + 1) * CHUNK, :
             ]
-        sum_send[d, 3 * CHUNK :, :] = jnp.zeros((2, 128), f32)
+        sum_send[d, 3 * CHUNK :, :] = packed[3 * BOX + d * REST_CHUNK : 3 * BOX + (d + 1) * REST_CHUNK, :]
     for d in range(1, DEPTH):
         t = lax.rem(z + d, DEPTH)
         c = remote(sum_send.at[t], sum_recv.at[z], sum_ss.at[t], sum_rs.at[z], at(me, t))
@@ -361,7 +401,11 @@
     power = sum_v[2 * CHUNK : 3 * CHUNK, :] + DAMPING
     obj_send[0:CHUNK, :] = sum_v[0:CHUNK, :] / power
     obj_send[CHUNK : 2 * CHUNK, :] = sum_v[CHUNK : 2 * CHUNK, :] / power
-    obj_send[2 * CHUNK :, :] = jnp.zeros((4, 128), f32)
+    rest = sum_v[3 * CHUNK :, :]
+    lane5 = lax.broadcasted_iota(jnp.int32, (REST_CHUNK, 128), 1)
+    power = jnp.where(lane5 < 2 * REST, pltpu.roll(rest, 128 - 4 * REST, 1), pltpu.roll(rest, 128 - 2 * REST, 1))
+    power = jnp.where(lane5 < 4 * REST, power, 0.0) + DAMPING
+    obj_send[2 * CHUNK :, :] = rest / power
     for d in range(1, DEPTH):
         t = lax.rem(z + d, DEPTH)
         c = remote(obj_send, obj_all.at[z], obj_ss.at[t], obj_rs.at[z], at(me, t))
@@ -372,24 +416,41 @@
         j = lax.rem(z + DEPTH - d, DEPTH)
         remote(obj_send, obj_all.at[j], obj_ss.at[j], obj_rs.at[j], at(me, j)).wait_recv()
     for d in range(DEPTH):
-        ore[d * CHUNK : d * CHUNK + CHUNK, :] = obj_all[d, 0:CHUNK, :]
-        oim[d * CHUNK : d * CHUNK + CHUNK, :] = obj_all[d, CHUNK : 2 * CHUNK, :]
-
-    r_at = lax.broadcasted_iota(jnp.int32, (SIDE, SIDE), 0)
-    c_at = lax.broadcasted_iota(jnp.int32, (SIDE, SIDE), 1)
-    flip_rows = jnp.where(lax.rem(r_at + c_at, SIDE) == 0, 1.0, 0.0).astype(bf16)
+        for part in range(2):
+            packed[part * BOX + d * CHUNK : part * BOX + (d + 1) * CHUNK, :] = obj_all[
+                d, part * CHUNK : (part + 1) * CHUNK, :
+            ]
+        packed[3 * BOX + d * REST_CHUNK : 3 * BOX + (d + 1) * REST_CHUNK, :] = obj_all[d, 2 * CHUNK :, :]
+    rest = packed[3 * BOX :, :]
+    for part, ref in enumerate((ore, oim)):
+        main = packed[part * BOX : (part + 1) * BOX, :]
+        for sign in range(2):
+            j = (2 * part + sign) * REST
+            x = stack(pltpu.roll(rest, (MAIN - j) % 128, 1), jnp.zeros((BOX - REST_ROWS, 128), f32))
+            x = jnp.where(lane80 < HALF, x, 0.0)
+            ref[sign * BOX : (sign + 1) * BOX, :] = jnp.where(
+                lane80 < MAIN, pltpu.roll(main, MAIN, 1) if sign else main, x
+            )
+
+    r_at = lax.broadcasted_iota(jnp.int32, (2 * SIDE, 2 * BOX), 0)
+    c_at = lax.broadcasted_iota(jnp.int32, (2 * SIDE, 2 * BOX), 1)
+    mirrored = r_at >= SIDE
+    k = jnp.where(mirrored, r_at - SIDE, r_at)
+    minus = (k >= HALF) != mirrored
+    k = jnp.where(k >= HALF, SIDE - k, k) + jnp.where(minus, BOX, 0)
+    pick_rows = jnp.where(k == c_at, 1.0, 0.0).astype(bf16)
     r_at = lax.broadcasted_iota(jnp.int32, (128, 256), 0)
     c_at = lax.broadcasted_iota(jnp.int32, (128, 256), 1)
     flip_columns = jnp.where(
         jnp.logical_and(r_at + c_at == SIDE, jnp.logical_and(c_at >= HALF, c_at < SIDE)), 1.0, 0.0
     ).astype(bf16)
-    parts = split(lanes(ore[...], oim[...]))
-    parts = [mm(flip_rows, part).astype(bf16) for part in parts]
+    parts = [mm(pick_rows, part) for part in split(lanes(ore[...], oim[...]))]
     lane_full = lax.broadcasted_iota(jnp.int32, (SIDE, 128), 1)
     for n, sign in ((0, 1.0), (1, -1.0)):
-        mirror = mm(parts[0][:, n * 128 : n * 128 + 128], flip_columns)
-        mirror = sign * (mirror + mm(parts[1][:, n * 128 : n * 128 + 128], flip_columns))
-        half = (ore, oim)[n][...]
+        at_n = slice(n * 128, n * 128 + 128)
+        half = parts[0][:SIDE, at_n] + parts[1][:SIDE, at_n]
+        mirror = [mm(part[SIDE:, at_n].astype(bf16), flip_columns) for part in parts]
+        mirror = sign * (mirror[0] + mirror[1])
         full[2 * n] = jnp.where(lane_full < HALF, half, mirror[:, :128])
         full[2 * n + 1] = mirror[:, 128:]
     first_row = z * 9 // 4
@@ -397,7 +458,7 @@
         placed = [jnp.zeros((8, 128), f32) for _ in range(6)]
         for t in range(3):
             for piece in range(2):
-                x = full[2 * n + piece, pl.ds(first_row + t, GROUP, stride=CHUNK), :]
+                x = full[2 * n + piece, pl.ds(first_row + t, GROUP, stride=SIDE // GROUP), :]
                 tile, off = divmod(SIDE * t + 128 * piece, 128)
                 if off:
                     x = pltpu.roll(x, off, 1)
@@ -420,24 +481,43 @@
 
     scale = 2.0 / (SIDE * SIDE)
 
-    def back(f, carry):
-        o_re, o_im, t_re, t_im = ore[...], oim[...], tre[f], tim[f]
-        e_re = dre[f] - (o_re * t_re - o_im * t_im)
-        e_im = dim_[f] - (o_re * t_im + o_im * t_re)
-        g_re = -scale * (e_re * o_re + e_im * o_im)
-        g_im = scale * (e_re * o_im - e_im * o_re)
-        y = mm3(table("left"), split(lanes(g_re, g_im)))
-        h = lanes(y[:SIDE, :128] - y[SIDE:, 128:], y[:SIDE, 128:] + y[SIDE:, :128])
-        focal = mm3(split(h), table("focal_right")) * (2.0 * intensity_scale)
-        g = jnp.concatenate([focal * fre[f], focal * fim[f]])
-        y = mm3(split(g[:, :SIDE]), table("back_right"))
-        q = lanes(y[:SIDE, :128] - y[SIDE:, 128:], y[:SIDE, 128:] + y[SIDE:, :128])
-        y = mm3(table("back_left"), split(q))
-        g_re, g_im = y[:BOX, :128] - y[BOX:, 128:], y[:BOX, 128:] + y[BOX:, :128]
-        dph[pl.ds(f, BOX, stride=GROUP), :] = of_frame(pre, f) * g_im - of_frame(pim, f) * g_re
+    def back(n, carry):
+        fs = [n * UNROLL + m for m in range(UNROLL)]
+        o_re, o_im = ore[...], oim[...]
+        h_re, h_im = [], []
+        for f in fs:
+            t_re, t_im = tre[f], tim[f]
+            e_re = dre[f] - (o_re * t_re - o_im * t_im)
+            e_im = dim_[f] - (o_re * t_im + o_im * t_re)
+            re_even, re_odd = fold(-scale * (e_re * o_re + e_im * o_im))
+            im_even, im_odd = fold(scale * (e_re * o_im - e_im * o_re))
+            c = mm3(table("focal_rows", 0, BOX), split(lanes(re_even, im_even)))
+            s = mm3(table("focal_rows", 128, BOX), split(lanes(re_odd, im_odd)))
+            cr, ci, sr, si = c[:, :128], c[:, 128:], s[:, :128], s[:, 128:]
+            h_re += [cr - si, cr + si]
+            h_im += [ci + sr, ci - sr]
+        even = mm3(both(stack(*h_re)), table("focal_columns", 0, 128)) * (4.0 * intensity_scale)
+        odd = mm3(both(stack(*h_im)), table("focal_columns", 128, 128)) * (4.0 * intensity_scale)
+        sum_rows, gap_rows = [], []
+        for m, f in enumerate(fs):
+            at_m = slice(2 * m * BOX, 2 * (m + 1) * BOX)
+            plus, minus = even[at_m] + odd[at_m], even[at_m] - odd[at_m]
+            p_re, p_im, m_re, m_im = plus * fpr[f], plus * fpi[f], minus * fmr[f], minus * fmi[f]
+            sum_rows += [p_re + m_re, p_im + m_im]
+            gap_rows += [p_re - m_re, p_im - m_im]
+        qc = mm3(both(stack(*sum_rows)), table("back_columns", 0, 128))
+        qs = mm3(both(stack(*gap_rows)), table("back_columns", 128, 128))
+        for m, f in enumerate(fs):
+            at_re, at_im = slice(4 * m * BOX, (4 * m + 2) * BOX), slice((4 * m + 2) * BOX, (4 * m + 4) * BOX)
+            re_even, re_odd = fold(qc[at_re] - qs[at_im])
+            im_even, im_odd = fold(qc[at_im] + qs[at_re])
+            c = mm3(table("back_rows", 0, BOX), split(lanes(re_even, im_even)))
+            s = mm3(table("back_rows", 128, BOX), split(lanes(re_odd, im_odd)))
+            g_re, g_im = c[:, :128] - s[:, 128:], c[:, 128:] + s[:, :128]
+            dph[pl.ds(f, BOX, stride=GROUP), :] = of_frame(pre, f) * g_im - of_frame(pim, f) * g_re
         return carry
 
-    lax.fori_loop(0, GROUP, back, 0)
+    lax.fori_loop(0, GROUP // UNROLL, back, 0)
 
     def project(g, total):
         tiles = [jnp.zeros((8, 128), f32) for _ in range(9)]
@@ -492,18 +572,17 @@
 
 
 def body(sky_image, coefficients, mode_basis, aperture):
-    window = np.broadcast_to((profile() / SIDE).astype(np.float32)[:, None], (SIDE, 128))
     vmem, dma = pltpu.VMEM, pltpu.SemaphoreType.DMA
     scratch = [
-        vmem(TABLE.shape, bf16), vmem((SIDE, 128), f32), vmem((640, 256), f32), vmem((GROUP, MODES), f32),
+        vmem(TABLE.shape, bf16), vmem((640, 256), f32), vmem((GROUP, MODES), f32),
         vmem((64, 128), f32), vmem((64, 128), f32), vmem((SIDE, SIDE), jnp.int32), vmem((MODES, FLAT), f32),
         vmem((3 * MODES, FLAT), bf16),
         vmem((4, 8, 640), f32), vmem((GROUP, SIDE, 128), f32), vmem((GROUP, 2, 8, 256), f32),
         vmem((GROUP, SIDE, 128), f32), vmem((8 * BOX, 128), f32), vmem((8 * BOX, 128), f32),
-        vmem((GROUP, SIDE, 256), f32), vmem((GROUP, SIDE, 256), f32),
-        *[vmem((GROUP, SIDE, 128), f32)] * 4,
-        vmem((3 * SIDE, 128), f32), vmem((DEPTH, 56, 128), f32), vmem((DEPTH, 56, 128), f32), vmem((56, 128), f32),
-        vmem((40, 128), f32), vmem((DEPTH, 40, 128), f32), vmem((SIDE, 128), f32), vmem((SIDE, 128), f32),
+        *[vmem((GROUP, 2 * BOX, 128), f32)] * 8,
+        vmem((3, 2 * BOX, 128), f32), vmem((3 * BOX + REST_ROWS, 128), f32),
+        vmem((DEPTH, SUMS, 128), f32), vmem((DEPTH, SUMS, 128), f32), vmem((SUMS, 128), f32),
+        vmem((OBJECTS, 128), f32), vmem((DEPTH, OBJECTS, 128), f32), vmem((2 * BOX, 128), f32), vmem((2 * BOX, 128), f32),
         vmem((8 * BOX, 128), f32), vmem((4, SIDE, 128), f32), vmem((GROUP, 8, 384), f32), vmem((GROUP, 8, 384), f32),
         vmem((8, 128), f32), vmem((DEPTH, 8, 128), f32), vmem((64, 128), f32), vmem((64, 128), f32),
         *[dma((8,))] * 19,
@@ -514,11 +593,11 @@
             jax.ShapeDtypeStruct((1, GROUP, MODES), f32),
             jax.ShapeDtypeStruct((GROUP, 2, SHARE), f32),
         ),
-        in_specs=[pl.BlockSpec(memory_space=pl.ANY)] * 6,
+        in_specs=[pl.BlockSpec(memory_space=pl.ANY)] * 5,
         out_specs=[pl.BlockSpec(memory_space=pltpu.VMEM)] * 2,
         scratch_shapes=scratch,
         compiler_params=pltpu.CompilerParams(collective_id=0, has_side_effects=True, vmem_limit_bytes=60 * 2**20),
-    )(sky_image, coefficients, mode_basis, aperture, jnp.asarray(TABLE), jnp.asarray(window))
+    )(sky_image, coefficients, mode_basis, aperture, jnp.asarray(TABLE))
 
 
 def solution(mesh):

time: 74.3 us -> 63.7 us (0.86)
  Pallas kernels: 69.2 us -> 59.9 us
  local copies, waits for them, and re-layouts: 4 us -> 2.62 us
    pallas_call x1, Pallas kernels: 69.2 us -> 59.9 us  [body(): pl.pallas_call(kernel, out_shape=(jax.ShapeDtypeStruct((1, GROUP, MODES),...]
    another operation x1 -> x0, local copies, waits for them, and re-layouts: 1.38 us -> none
where the time goes in v2:
time: 63.7 us; the launch traced here: 63.2 us
  Pallas kernels  59.9 us (94%)
  local copies, waits for them, and re-layouts  2.62 us (4%)
  between operations  0.64 us (1%)
    pallas_call x1, Pallas kernels, body(): pl.pallas_call(kernel, out_shape=(jax.ShapeDtypeStruct((1, GROUP, MODES),...  59.9 us
    unnamed x2, local copies, waits for them, and re-layouts  2.62 us

profile of v2, /device:TPU:4, one launch (start us, length us, event | category | flops | bytes accessed | tf_op | source)
XLA Modules:
  0.0 63.2 jit_solution(16471980488680445350)
XLA Ops:
  0.6 59.9 %shard_map.68 = (f32[1,8,64]{2,1,0:T(8,128)}, f32[8,2,324]{2,1,0:T(2,128)}) custom-call(f32[1,512,256]{2,1,0:T(8,128)} %sky.1, f32[1,8,64]{2,1,0:T(8,128)} %coef.1, f32[64,20736]{1,0:T(8,128)} %basis.1, s32[144,144]{1,0:T(8,128)} %aperture.1, bf16[2,864,256]{2,1,0:T(8,128)(2,1)} %constant.2.clone.table_hbm), custom_call_target="tpu_custom_call" | custom-call | tf_op jit(solution)/shard_map/pallas_call | solution.py:590
  60.6 1.3 %copy.9 = f32[1,8,64]{2,1,0:T(8,128)} copy(f32[1,8,64]{2,1,0:T(8,128)} %get-tuple-element.4) | data formatting | bytes 4096
  61.8 1.4 %copy.10 = f32[8,2,324]{2,1,0:T(2,128)} copy(f32[8,2,324]{2,1,0:T(2,128)} %get-tuple-element.5) | data formatting | bytes 41472

commit v3 on v2

--- a/solution.py
+++ b/solution.py
@@ -27,7 +27,7 @@
 FLAT = BOX * SIDE
 PERIOD = 8 * SIDE
 MODES = 64
-UNROLL = 2
+UNROLL = GROUP
 SHARE = SIDE * SIDE // FRAMES
 DAMPING = 0.02 * FRAMES
 MESH = pl.DeviceIdType.MESH
@@ -52,39 +52,53 @@
         angle = 2.0 * math.pi / SIDE * (np.outer(a, b) % SIDE)
         return np.cos(angle), np.sin(angle)
 
-    def beside(c, s):
+    def cut(t):
+        high = t.astype(ml_dtypes.bfloat16)
+        return high, (t - high.astype(np.float64)).astype(ml_dtypes.bfloat16)
+
+    def rows_of(*blocks):
+        t = np.zeros((BOX * len(blocks), blocks[0].shape[1]))
+        for n, block in enumerate(blocks):
+            t[n * BOX : n * BOX + block.shape[0]] = block
+        high, low = cut(t)
+        return np.concatenate([high, high, low], axis=1)
+
+    def columns_of(c, s):
         t = np.zeros((-(-c.shape[0] // 16) * 16, 256))
         t[: c.shape[0], : c.shape[1]], t[: c.shape[0], 128 : 128 + c.shape[1]] = c, s
-        return t
-
-    def below(c, s):
-        t = np.zeros((2 * BOX, 256))
-        t[:HALF, : c.shape[1]], t[BOX : BOX + HALF, : c.shape[1]] = c, s
-        return t
+        return cut(t)
+
+    def twice(c, s):
+        high, low = columns_of(c, s)
+        return np.concatenate([high, np.zeros((128 - BOX, 256), high.dtype), high]), low
 
     parts = {}
     c, s = pair(k, u)
-    parts["pupil_rows"] = below(c, s)
-    parts["pupil_columns"] = beside(c.T, s.T)
-    parts["back_columns"] = beside(weight[:, None] * c, weight[:, None] * s)
-    parts["back_rows"] = beside(c.T * weight, s.T * weight)
+    parts["pupil_rows"] = rows_of(c, s)
+    parts["pupil_columns"], parts["pupil_columns_low"] = twice(c.T, s.T)
+    parts["back_columns"], parts["back_columns_low"] = twice(weight[:, None] * c, weight[:, None] * s)
+
+    def wide(t):
+        return np.pad(t, ((0, BOX - t.shape[0]), (0, BOX - t.shape[1])))
+
+    parts["back_even"], parts["back_odd"] = rows_of(wide(c.T * weight)), rows_of(wide(s.T * weight))
     c, s = pair(k, k)
-    parts["focal_columns"] = beside(weight[:, None] * c, -weight[:, None] * s)
-    parts["focal_rows"] = beside(c * weight, s * weight)
+    parts["focal_columns"], parts["focal_columns_low"] = twice(weight[:, None] * c, -weight[:, None] * s)
+    parts["focal_even"], parts["focal_odd"] = rows_of(wide(c * weight)), rows_of(wide(s * weight))
     w = profile()
     c, s = pair(k, y)
-    parts["data_rows"] = below(c * w / SIDE, s * w / SIDE)
+    t = rows_of(c * w / SIDE, s * w / SIDE)
+    parts["data_rows"], parts["data_rows_end"] = t[:, :256], t[:, 256:]
     order = np.concatenate([y[RIM:-RIM], y[:RIM], y[-RIM:]])
-    parts["data_columns"] = beside((w[:, None] * c.T)[order], -(w[:, None] * s.T)[order])
+    parts["data_columns"], parts["data_columns_low"] = columns_of(
+        (w[:, None] * c.T)[order], -(w[:, None] * s.T)[order]
+    )
     first, rows, total = {}, [], 0
     for name, part in parts.items():
-        first[name] = (total, part.shape[0])
+        first[name] = (total, *part.shape)
         total += part.shape[0]
-        rows.append(part)
-    whole = np.concatenate(rows)
-    high = whole.astype(ml_dtypes.bfloat16)
-    rest = (whole - high.astype(np.float64)).astype(ml_dtypes.bfloat16)
-    return np.stack([high, rest]), first
+        rows.append(np.pad(part, ((0, 0), (0, 256 - part.shape[1]))))
+    return np.concatenate(rows), first
 
 
 TABLE, FIRST = tables()
@@ -146,9 +160,19 @@
             src_ref=src, dst_ref=dst, send_sem=send, recv_sem=recv, device_id=device, device_id_type=MESH
         )
 
-    def table(name, start, width):
-        row, count = FIRST[name]
-        return tuple(tab[n, row : row + count, start : start + width] for n in range(2))
+    def table(name, half=None):
+        row, count, width = FIRST[name]
+        if half is None:
+            return tab[row : row + count, :width]
+        return tab[row : row + count, half * 128 : half * 128 + 128]
+
+    def from_left(name, x):
+        h, r = split(x)
+        return mm(table(name), jnp.concatenate([h, r, h]))
+
+    def from_right(x, name, half=None):
+        h, r = split(x)
+        return mm(lanes(h, r)[:, : 128 + BOX], table(name, half)) + mm(h[:, :BOX], table(name + "_low", half))
 
     loads = [
         pltpu.make_async_copy(coef.at[0], coef_v, local_sem.at[0]),
@@ -284,17 +308,13 @@
         pim[at_g, :] = m * sine
         return carry
 
-    lax.fori_loop(0, BOX // 8, pupils, 0)
+    lax.fori_loop(0, BOX // 8, pupils, 0, unroll=2)
 
     def of_frame(ref, f):
         return ref[pl.ds(f, BOX, stride=GROUP), :]
 
     def fold(x):
         return x[:BOX] + x[BOX:], x[:BOX] - x[BOX:]
-
-    def both(x):
-        h, r = split(x)
-        return h[:, :BOX], r[:, :BOX]
 
     def stack(*parts):
         return jnp.concatenate(parts)
@@ -303,10 +323,10 @@
         fs = [n * UNROLL + m for m in range(UNROLL)]
         rows = []
         for f in fs:
-            y = mm3(table("pupil_rows", 0, BOX), split(lanes(of_frame(pre, f), of_frame(pim, f))))
+            y = from_left("pupil_rows", lanes(of_frame(pre, f), of_frame(pim, f)))
             cr, ci, sr, si = y[:BOX, :128], y[:BOX, 128:], y[BOX:, :128], y[BOX:, 128:]
             rows += [cr + si, cr - si, ci - sr, ci + sr]
-        y = mm3(both(stack(*rows)), table("pupil_columns", 0, 256))
+        y = from_right(stack(*rows), "pupil_columns")
         even, odd = [], []
         for m, f in enumerate(fs):
             r, i = y[4 * m * BOX : (4 * m + 2) * BOX], y[(4 * m + 2) * BOX : (4 * m + 4) * BOX]
@@ -317,12 +337,12 @@
             minus = (m_re * m_re + m_im * m_im) * intensity_scale
             even += fold(plus + minus)
             odd += fold(plus - minus)
-        x_re = mm3(both(stack(*even)), table("focal_columns", 0, 128))
-        x_im = mm3(both(stack(*odd)), table("focal_columns", 128, 128))
+        x_re = from_right(stack(*even), "focal_columns", 0)
+        x_im = from_right(stack(*odd), "focal_columns", 1)
         for m, f in enumerate(fs):
             x = lanes(x_re[2 * m * BOX : 2 * (m + 1) * BOX], x_im[2 * m * BOX : 2 * (m + 1) * BOX])
-            c = mm3(table("focal_rows", 0, BOX), split(x[:BOX]))
-            s = mm3(table("focal_rows", 128, BOX), split(x[BOX:]))
+            c = from_left("focal_even", x[:BOX])
+            s = from_left("focal_odd", x[BOX:])
             cr, ci, sr, si = c[:, :128], c[:, 128:], s[:, :128], s[:, 128:]
             tre[f] = stack(cr + si, cr - si)
             tim[f] = stack(ci - sr, ci + sr)
@@ -351,10 +371,12 @@
     def data(n, carry):
         fs = [n * UNROLL + m for m in range(UNROLL)]
         h, r = split(stack(*[lanes(img[f], turned[f]) for f in fs]))
-        x = mm3((h[:, :SIDE], r[:, :SIDE]), table("data_columns", 0, 256))
+        x = mm3((h[:, :SIDE], r[:, :SIDE]), (table("data_columns"), table("data_columns_low")))
         n_re, n_im, power = sums[0], sums[1], sums[2]
         for m, f in enumerate(fs):
-            y = mm3(table("data_rows", 0, SIDE), split(x[m * SIDE : (m + 1) * SIDE]))
+            h, r = split(x[m * SIDE : (m + 1) * SIDE])
+            h = stack(h, r, h)
+            y = mm(table("data_rows"), h[:256]) + mm(table("data_rows_end"), h[256:])
             cr, ci, sr, si = y[:BOX, :128], y[:BOX, 128:], y[BOX:, :128], y[BOX:, 128:]
             d_re, d_im = stack(cr + si, cr - si), stack(ci - sr, ci + sr)
             dre[f] = d_re
@@ -431,6 +453,72 @@
             ref[sign * BOX : (sign + 1) * BOX, :] = jnp.where(
                 lane80 < MAIN, pltpu.roll(main, MAIN, 1) if sign else main, x
             )
+
+    scale = 2.0 / (SIDE * SIDE)
+
+    def back(n, carry):
+        fs = [n * UNROLL + m for m in range(UNROLL)]
+        o_re, o_im = ore[...], oim[...]
+        h_re, h_im = [], []
+        for f in fs:
+            t_re, t_im = tre[f], tim[f]
+            e_re = dre[f] - (o_re * t_re - o_im * t_im)
+            e_im = dim_[f] - (o_re * t_im + o_im * t_re)
+            re_even, re_odd = fold(-scale * (e_re * o_re + e_im * o_im))
+            im_even, im_odd = fold(scale * (e_re * o_im - e_im * o_re))
+            c = from_left("focal_even", lanes(re_even, im_even))
+            s = from_left("focal_odd", lanes(re_odd, im_odd))
+            cr, ci, sr, si = c[:, :128], c[:, 128:], s[:, :128], s[:, 128:]
+            h_re += [cr - si, cr + si]
+            h_im += [ci + sr, ci - sr]
+        even = from_right(stack(*h_re), "focal_columns", 0) * (4.0 * intensity_scale)
+        odd = from_right(stack(*h_im), "focal_columns", 1) * (4.0 * intensity_scale)
+        sum_rows, gap_rows = [], []
+        for m, f in enumerate(fs):
+            at_m = slice(2 * m * BOX, 2 * (m + 1) * BOX)
+            plus, minus = even[at_m] + odd[at_m], even[at_m] - odd[at_m]
+            p_re, p_im, m_re, m_im = plus * fpr[f], plus * fpi[f], minus * fmr[f], minus * fmi[f]
+            sum_rows += [p_re + m_re, p_im + m_im]
+            gap_rows += [p_re - m_re, p_im - m_im]
+        qc = from_right(stack(*sum_rows), "back_columns", 0)
+        qs = from_right(stack(*gap_rows), "back_columns", 1)
+        for m, f in enumerate(fs):
+            at_re, at_im = slice(4 * m * BOX, (4 * m + 2) * BOX), slice((4 * m + 2) * BOX, (4 * m + 4) * BOX)
+            re_even, re_odd = fold(qc[at_re] - qs[at_im])
+            im_even, im_odd = fold(qc[at_im] + qs[at_re])
+            c = from_left("back_even", lanes(re_even, im_even))
+            s = from_left("back_odd", lanes(re_odd, im_odd))
+            g_re, g_im = c[:, :128] - s[:, 128:], c[:, 128:] + s[:, :128]
+            dph[pl.ds(f, BOX, stride=GROUP), :] = of_frame(pre, f) * g_im - of_frame(pim, f) * g_re
+        return carry
+
+    lax.fori_loop(0, GROUP // UNROLL, back, 0)
+
+    def project(g, total):
+        tiles = [jnp.zeros((8, 128), f32) for _ in range(9)]
+        for r, (tile, off) in enumerate(starts):
+            x = dph[pl.ds(pl.multiple_of(g * 64, 64) + 8 * r, 8), :]
+            if off:
+                x = pltpu.roll(x, off, 1)
+            if off + BOX > 128:
+                tiles[tile + 1] += jnp.where(lane < off, x, 0.0)
+                x = jnp.where(lane < off, 0.0, x)
+            tiles[tile] += x
+        x = jnp.concatenate(split(lanes(*tiles)))
+        modes = base3[0 : 2 * MODES, pl.ds(pl.multiple_of(g * PERIOD, 128), PERIOD)]
+        return total + lax.dot_general(x, modes, (((1,), (1,)), ((), ())), preferred_element_type=f32)
+
+    total = lax.fori_loop(0, BOX // 8, project, jnp.zeros((16, 128), f32), unroll=5)
+    total = total[:8] + total[8:]
+    gradient = total + pltpu.roll(total, MODES, 1)
+
+    grad_send[...] = gradient
+    for d in range(1, DEPTH):
+        t = lax.rem(z + d, DEPTH)
+        c = remote(grad_send, grad_recv.at[z], grad_ss.at[t], grad_rs.at[z], at(me, t))
+        c.start()
+        sends.append(c)
+    grad_recv[z] = gradient
 
     r_at = lax.broadcasted_iota(jnp.int32, (2 * SIDE, 2 * BOX), 0)
     c_at = lax.broadcasted_iota(jnp.int32, (2 * SIDE, 2 * BOX), 1)
@@ -479,71 +567,6 @@
         sends.append(c)
     out_recv[me] = out_send[me]
 
-    scale = 2.0 / (SIDE * SIDE)
-
-    def back(n, carry):
-        fs = [n * UNROLL + m for m in range(UNROLL)]
-        o_re, o_im = ore[...], oim[...]
-        h_re, h_im = [], []
-        for f in fs:
-            t_re, t_im = tre[f], tim[f]
-            e_re = dre[f] - (o_re * t_re - o_im * t_im)
-            e_im = dim_[f] - (o_re * t_im + o_im * t_re)
-            re_even, re_odd = fold(-scale * (e_re * o_re + e_im * o_im))
-            im_even, im_odd = fold(scale * (e_re * o_im - e_im * o_re))
-            c = mm3(table("focal_rows", 0, BOX), split(lanes(re_even, im_even)))
-            s = mm3(table("focal_rows", 128, BOX), split(lanes(re_odd, im_odd)))
-            cr, ci, sr, si = c[:, :128], c[:, 128:], s[:, :128], s[:, 128:]
-            h_re += [cr - si, cr + si]
-            h_im += [ci + sr, ci - sr]
-        even = mm3(both(stack(*h_re)), table("focal_columns", 0, 128)) * (4.0 * intensity_scale)
-        odd = mm3(both(stack(*h_im)), table("focal_columns", 128, 128)) * (4.0 * intensity_scale)
-        sum_rows, gap_rows = [], []
-        for m, f in enumerate(fs):
-            at_m = slice(2 * m * BOX, 2 * (m + 1) * BOX)
-            plus, minus = even[at_m] + odd[at_m], even[at_m] - odd[at_m]
-            p_re, p_im, m_re, m_im = plus * fpr[f], plus * fpi[f], minus * fmr[f], minus * fmi[f]
-            sum_rows += [p_re + m_re, p_im + m_im]
-            gap_rows += [p_re - m_re, p_im - m_im]
-        qc = mm3(both(stack(*sum_rows)), table("back_columns", 0, 128))
-        qs = mm3(both(stack(*gap_rows)), table("back_columns", 128, 128))
-        for m, f in enumerate(fs):
-            at_re, at_im = slice(4 * m * BOX, (4 * m + 2) * BOX), slice((4 * m + 2) * BOX, (4 * m + 4) * BOX)
-            re_even, re_odd = fold(qc[at_re] - qs[at_im])
-            im_even, im_odd = fold(qc[at_im] + qs[at_re])
-            c = mm3(table("back_rows", 0, BOX), split(lanes(re_even, im_even)))
-            s = mm3(table("back_rows", 128, BOX), split(lanes(re_odd, im_odd)))
-            g_re, g_im = c[:, :128] - s[:, 128:], c[:, 128:] + s[:, :128]
-            dph[pl.ds(f, BOX, stride=GROUP), :] = of_frame(pre, f) * g_im - of_frame(pim, f) * g_re
-        return carry
-
-    lax.fori_loop(0, GROUP // UNROLL, back, 0)
-
-    def project(g, total):
-        tiles = [jnp.zeros((8, 128), f32) for _ in range(9)]
-        for r, (tile, off) in enumerate(starts):
-            x = dph[pl.ds(pl.multiple_of(g * 64, 64) + 8 * r, 8), :]
-            if off:
-                x = pltpu.roll(x, off, 1)
-            if off + BOX > 128:
-                tiles[tile + 1] += jnp.where(lane < off, x, 0.0)
-                x = jnp.where(lane < off, 0.0, x)
-            tiles[tile] += x
-        x = jnp.concatenate(split(lanes(*tiles)))
-        modes = base3[0 : 2 * MODES, pl.ds(pl.multiple_of(g * PERIOD, 128), PERIOD)]
-        return total + lax.dot_general(x, modes, (((1,), (1,)), ((), ())), preferred_element_type=f32)
-
-    total = lax.fori_loop(0, BOX // 8, project, jnp.zeros((16, 128), f32))
-    total = total[:8] + total[8:]
-    gradient = total + pltpu.roll(total, MODES, 1)
-
-    grad_send[...] = gradient
-    for d in range(1, DEPTH):
-        t = lax.rem(z + d, DEPTH)
-        c = remote(grad_send, grad_recv.at[z], grad_ss.at[t], grad_rs.at[z], at(me, t))
-        c.start()
-        sends.append(c)
-    grad_recv[z] = gradient
     for d in range(1, DEPTH):
         j = lax.rem(z + DEPTH - d, DEPTH)
         remote(grad_send, grad_recv.at[j], grad_ss.at[j], grad_rs.at[j], at(me, j)).wait_recv()

time: 63.7 us -> 52.5 us (0.82)
  the two profiles are of different devices: /device:TPU:4 before, /device:TPU:2 now
where the time goes in v3:
time: 52.5 us; the launch traced here: 52.3 us
  Pallas kernels  49 us (93%)
  local copies, waits for them, and re-layouts  2.62 us (5%)
  between operations  0.64 us (1%)
    pallas_call x1, Pallas kernels, body(): pl.pallas_call(kernel, out_shape=(jax.ShapeDtypeStruct((1, GROUP, MODES),...  49 us
    unnamed x2, local copies, waits for them, and re-layouts  2.62 us

profile of v3, /device:TPU:2, one launch (start us, length us, event | category | flops | bytes accessed | tf_op | source)
XLA Modules:
  0.0 52.3 jit_solution(14593204984352190050)
XLA Ops:
  0.6 49.0 %shard_map.68 = (f32[1,8,64]{2,1,0:T(8,128)}, f32[8,2,324]{2,1,0:T(2,128)}) custom-call(f32[1,512,256]{2,1,0:T(8,128)} %sky.1, f32[1,8,64]{2,1,0:T(8,128)} %coef.1, f32[64,20736]{1,0:T(8,128)} %basis.1, s32[144,144]{1,0:T(8,128)} %aperture.1, bf16[1952,256]{1,0:T(8,128)(2,1)} %constant.2.clone.table_hbm), custom_call_target="tpu_custom_call" | custom-call | tf_op jit(solution)/shard_map/pallas_call | solution.py:613
  49.7 1.3 %copy.9 = f32[1,8,64]{2,1,0:T(8,128)} copy(f32[1,8,64]{2,1,0:T(8,128)} %get-tuple-element.4) | data formatting | bytes 4096
  51.0 1.4 %copy.10 = f32[8,2,324]{2,1,0:T(2,128)} copy(f32[8,2,324]{2,1,0:T(2,128)} %get-tuple-element.5) | data formatting | bytes 41472

commit v4 on v3

--- a/solution.py
+++ b/solution.py
@@ -145,12 +145,19 @@
     tab, skyp, coef_v, coef_send, coef_recv, mask_v, base, base3,
     edges, img, halo, turned, pre, pim, fpr, fpi, fmr, fmi, tre, tim, dre, dim_,
     sums, packed, sum_send, sum_recv, sum_v, obj_send, obj_all, ore, oim, dph,
-    full, out_send, out_recv, grad_send, grad_recv, ret_send, ret_recv,
+    full, out_send, out_recv, part_send, part_recv, ret_send, ret_recv,
     local_sem, coef_ss, coef_rs, img_ss, img_rs, own_ss, own_rs, cross_ss, cross_rs,
-    sum_ss, sum_rs, obj_ss, obj_rs, out_ss, out_rs, grad_ss, grad_rs, ret_ss, ret_rs,
+    sum_ss, sum_rs, obj_ss, obj_rs, out_ss, out_rs, ret_ss, ret_rs, part_sem,
 ):
     place, strip = lax.axis_index("frame"), lax.axis_index("patch")
     me, z = place // DEPTH, place % DEPTH
+
+    y, x = me // 2, me % 2
+    other = 1 - x
+    near, far, back_y = y + 1 - 2 * (y % 2), 3 - y, (y + 2) % 4
+    close = [near * 2 + x, far * 2 + x, y * 2 + other]
+    distant = [near * 2 + other, far * 2 + other, back_y * 2 + x, back_y * 2 + other]
+    peers = distant[::-1] + close[::-1]
 
     def at(group, depth, which=None):
         return {"frame": group * DEPTH + depth, "patch": strip if which is None else which}
@@ -190,8 +197,8 @@
     def greet(device):
         pl.semaphore_signal(barrier, inc=1, device_id=device, device_id_type=MESH)
 
-    for d in range(1, GROUP):
-        greet(at(lax.rem(me + d, GROUP), z))
+    for t in peers:
+        greet(at(t, z))
     for d in range(1, DEPTH):
         greet(at(me, lax.rem(z + d, DEPTH)))
     for j in range(GROUP):
@@ -214,8 +221,7 @@
     def rows8(ref, j):
         return ref.at[pl.ds(pl.multiple_of(j * 8, 8), 8)]
 
-    for d in range(1, GROUP):
-        t = lax.rem(me + d, GROUP)
+    for t in peers:
         c = remote(rows8(coef_send, t), rows8(coef_recv, me), coef_ss.at[t], coef_rs.at[me], at(t, z))
         c.start()
         sends.append(c)
@@ -229,11 +235,7 @@
     def edge_of(kind, t):
         return edges.at[kind, :, pl.ds(pl.multiple_of(lax.rem(t, 4) * TILE, TILE), 256)]
 
-    for d in range(1, GROUP):
-        t = lax.rem(me + d, GROUP)
-        c = remote(main_of(t), img.at[me], img_ss.at[t], img_rs.at[me], at(t, z))
-        c.start()
-        sends.append(c)
+    for t in peers:
         kind, side = jnp.where(t < 4, 2, 1), jnp.where(t < 4, 1, 0)
         c = remote(edge_of(kind, t), halo.at[me, side], own_ss.at[t], own_rs.at[me], at(t, z))
         c.start()
@@ -244,6 +246,10 @@
             edge_of(kind, p), halo.at[me, side], cross_ss.at[p], cross_rs.at[me],
             at(p, z, lax.rem(strip + step, STRIPS)),
         )
+        c.start()
+        sends.append(c)
+    for t in close + distant:
+        c = remote(main_of(t), img.at[me], img_ss.at[t], img_rs.at[me], at(t, z))
         c.start()
         sends.append(c)
     own_side = jnp.where(me < 4, 1, 0)
@@ -277,8 +283,7 @@
     intensity_scale = 1.0 / (SIDE * SIDE * area)
     dph[0:BOX, :] = mask
 
-    for d in range(1, GROUP):
-        j = lax.rem(me + GROUP - d, GROUP)
+    for j in peers:
         remote(rows8(coef_send, j), rows8(coef_recv, j), coef_ss.at[j], coef_rs.at[j], at(j, z)).wait_recv()
     weights = coef_recv[pl.ds(0, GROUP, stride=8), :]
     w0 = weights.astype(bf16).astype(f32)
@@ -354,9 +359,7 @@
         c.wait()
     for j in range(GROUP):
         remote(edge_of(0, 0), halo.at[j, 1 - own_side], cross_ss.at[j], cross_rs.at[j], at(j, z, beside)).wait_recv()
-    for d in range(1, GROUP):
-        j = lax.rem(me + GROUP - d, GROUP)
-        remote(main_of(j), img.at[j], img_ss.at[j], img_rs.at[j], at(j, z)).wait_recv()
+    for j in peers:
         remote(edge_of(0, j), halo.at[j, own_side], own_ss.at[j], own_rs.at[j], at(j, z)).wait_recv()
     row = lax.broadcasted_iota(jnp.int32, (128, 256), 0)
     left_on = jnp.where(jnp.logical_and(strip == 0, me < 4), 0.0, 1.0)
@@ -368,8 +371,7 @@
 
     sums[...] = jnp.zeros_like(sums)
 
-    def data(n, carry):
-        fs = [n * UNROLL + m for m in range(UNROLL)]
+    def data(fs):
         h, r = split(stack(*[lanes(img[f], turned[f]) for f in fs]))
         x = mm3((h[:, :SIDE], r[:, :SIDE]), (table("data_columns"), table("data_columns_low")))
         n_re, n_im, power = sums[0], sums[1], sums[2]
@@ -386,9 +388,15 @@
             n_im = n_im + (t_re * d_im - t_im * d_re)
             power = power + (t_re * t_re + t_im * t_im)
         sums[0], sums[1], sums[2] = n_re, n_im, power
-        return carry
-
-    lax.fori_loop(0, GROUP // UNROLL, data, 0)
+
+    def arrive(js):
+        for j in js:
+            remote(main_of(j), img.at[j], img_ss.at[j], img_rs.at[j], at(j, z)).wait_recv()
+
+    arrive(close)
+    data([me, *close])
+    arrive(distant)
+    data(distant)
 
     lane80 = lax.broadcasted_iota(jnp.int32, (BOX, 128), 1)
     lane40 = lax.broadcasted_iota(jnp.int32, (REST_ROWS, 128), 1)
@@ -512,13 +520,21 @@
     total = total[:8] + total[8:]
     gradient = total + pltpu.roll(total, MODES, 1)
 
-    grad_send[...] = gradient
-    for d in range(1, DEPTH):
-        t = lax.rem(z + d, DEPTH)
-        c = remote(grad_send, grad_recv.at[z], grad_ss.at[t], grad_rs.at[z], at(me, t))
-        c.start()
-        sends.append(c)
-    grad_recv[z] = gradient
+    for j in range(GROUP):
+        ret_send[j] = gradient[j : j + 1]
+    part_send[0] = jnp.sum(gradient, axis=0, keepdims=True)
+
+    groups = list(zip([*peers, me], (3, 2, 2, 2, 1, 1, 1, 0)))
+    depths = [(z, 0)] + [(lax.rem(z + d, DEPTH), min(d, DEPTH - d)) for d in range(1, DEPTH)]
+    ways = [(a + b, group, depth) for group, a in groups for depth, b in depths if a + b]
+    for _, group, depth in sorted(ways, key=lambda way: -way[0]):
+        remote(part_send, part_recv.at[pl.ds(place, 1)], part_sem.at[0], part_sem.at[1], at(group, depth)).start()
+    for t in peers:
+        c = remote(ret_send.at[t], ret_recv.at[me], ret_ss.at[t], ret_rs.at[me], at(t, z))
+        c.start()
+        sends.append(c)
+    part_recv[place] = part_send[0]
+    ret_recv[me] = ret_send[me]
 
     r_at = lax.broadcasted_iota(jnp.int32, (2 * SIDE, 2 * BOX), 0)
     c_at = lax.broadcasted_iota(jnp.int32, (2 * SIDE, 2 * BOX), 1)
@@ -560,36 +576,27 @@
             picked = picked + jnp.where(lax.rem(z, 4) == m, 1.0, 0.0) * moved[:, :384]
         for i in range(GROUP):
             out_send[i, n : n + 1, :] = picked[i : i + 1]
-    for d in range(1, GROUP):
-        t = lax.rem(me + d, GROUP)
+    for t in peers:
         c = remote(out_send.at[t], out_recv.at[me], out_ss.at[t], out_rs.at[me], at(t, z))
         c.start()
         sends.append(c)
     out_recv[me] = out_send[me]
 
-    for d in range(1, DEPTH):
-        j = lax.rem(z + DEPTH - d, DEPTH)
-        remote(grad_send, grad_recv.at[j], grad_ss.at[j], grad_rs.at[j], at(me, j)).wait_recv()
-    mean = jnp.sum(grad_recv[...].reshape(64, 128), axis=0, keepdims=True) * (1.0 / FRAMES)
-    gradient = gradient - mean
-    for j in range(GROUP):
-        ret_send[8 * j : 8 * j + 8, :] = jnp.broadcast_to(gradient[j : j + 1], (8, 128))
-    for d in range(1, GROUP):
-        t = lax.rem(me + d, GROUP)
-        c = remote(rows8(ret_send, t), rows8(ret_recv, me), ret_ss.at[t], ret_rs.at[me], at(t, z))
-        c.start()
-        sends.append(c)
-    ret_recv[pl.ds(pl.multiple_of(me * 8, 8), 8), :] = ret_send[pl.ds(pl.multiple_of(me * 8, 8), 8), :]
-
-    for d in range(1, GROUP):
-        j = lax.rem(me + GROUP - d, GROUP)
+    for j in peers:
         remote(out_send.at[j], out_recv.at[j], out_ss.at[j], out_rs.at[j], at(j, z)).wait_recv()
     for p in range(GROUP):
         object_out[p] = out_recv[p, 0:2, :SHARE]
-    for d in range(1, GROUP):
-        j = lax.rem(me + GROUP - d, GROUP)
-        remote(rows8(ret_send, j), rows8(ret_recv, j), ret_ss.at[j], ret_rs.at[j], at(j, z)).wait_recv()
-    gradient_out[0] = ret_recv[pl.ds(0, GROUP, stride=8), :][:, :MODES]
+    for j in peers:
+        remote(ret_send.at[j], ret_recv.at[j], ret_ss.at[j], ret_rs.at[j], at(j, z)).wait_recv()
+    arrived = part_recv.at[pl.ds(0, FRAMES - 1)]
+    arrived = remote(arrived, arrived, part_sem.at[0], part_sem.at[1], at(peers[0], z))
+    arrived.wait_recv()
+    for p in range(GROUP):
+        mean = part_recv[p * DEPTH]
+        for n in range(1, DEPTH):
+            mean = mean + part_recv[p * DEPTH + n]
+        gradient_out[0, p : p + 1, :] = (ret_recv[p] - mean * (1.0 / FRAMES))[:, :MODES]
+    arrived.wait_send()
     for c in sends:
         c.wait_send()
 
@@ -607,14 +614,14 @@
         vmem((DEPTH, SUMS, 128), f32), vmem((DEPTH, SUMS, 128), f32), vmem((SUMS, 128), f32),
         vmem((OBJECTS, 128), f32), vmem((DEPTH, OBJECTS, 128), f32), vmem((2 * BOX, 128), f32), vmem((2 * BOX, 128), f32),
         vmem((8 * BOX, 128), f32), vmem((4, SIDE, 128), f32), vmem((GROUP, 8, 384), f32), vmem((GROUP, 8, 384), f32),
-        vmem((8, 128), f32), vmem((DEPTH, 8, 128), f32), vmem((64, 128), f32), vmem((64, 128), f32),
-        *[dma((8,))] * 19,
+        vmem((1, 1, 128), f32), vmem((FRAMES, 1, 128), f32), vmem((GROUP, 1, 128), f32), vmem((GROUP, 1, 128), f32),
+        *[dma((8,))] * 17, dma((2,)),
     ]
     return pl.pallas_call(
         kernel,
         out_shape=(
-            jax.ShapeDtypeStruct((1, GROUP, MODES), f32),
-            jax.ShapeDtypeStruct((GROUP, 2, SHARE), f32),
+            pltpu.VMEM((1, GROUP, MODES), f32),
+            pltpu.VMEM((GROUP, 2, SHARE), f32),
         ),
         in_specs=[pl.BlockSpec(memory_space=pl.ANY)] * 5,
         out_specs=[pl.BlockSpec(memory_space=pltpu.VMEM)] * 2,

time: 52.5 us -> 46.5 us (0.89)
  the two profiles are of different devices: /device:TPU:2 before, /device:TPU:4 now
where the time goes in v4:
time: 46.5 us; the launch traced here: 46.4 us
  Pallas kernels  44.6 us (96%)
  local copies, waits for them, and re-layouts  1.2 us (3%)
  between operations  0.64 us (1%)
    pallas_call x1, Pallas kernels, body(): pl.pallas_call(kernel, out_shape=(pltpu.VMEM((1, GROUP, MODES), f32), plt...  44.6 us
    unnamed x2, local copies, waits for them, and re-layouts  1.2 us

profile of v4, /device:TPU:4, one launch (start us, length us, event | category | flops | bytes accessed | tf_op | source)
XLA Modules:
  0.0 46.4 jit_solution(3384962102365216095)
XLA Ops:
  0.6 44.6 %shard_map.68 = (f32[1,8,64]{2,1,0:T(8,128)S(1)}, f32[8,2,324]{2,1,0:T(2,128)S(1)}) custom-call(f32[1,512,256]{2,1,0:T(8,128)} %sky.1, f32[1,8,64]{2,1,0:T(8,128)} %coef.1, f32[64,20736]{1,0:T(8,128)} %basis.1, s32[144,144]{1,0:T(8,128)} %aperture.1, bf16[1952,256]{1,0:T(8,128)(2,1)} %constant.2.clone.table_hbm), custom_call_target="tpu_custom_call" | custom-call | tf_op jit(solution)/shard_map/pallas_call | solution.py:620
  45.2 0.6 %copy.9 = f32[1,8,64]{2,1,0:T(8,128)} copy(f32[1,8,64]{2,1,0:T(8,128)S(1)} %get-tuple-element.2) | data formatting | bytes 4096
  45.8 0.6 %copy.10 = f32[8,2,324]{2,1,0:T(2,128)} copy(f32[8,2,324]{2,1,0:T(2,128)S(1)} %get-tuple-element.3) | data formatting | bytes 41472

commit v5 on v4

--- a/solution.py
+++ b/solution.py
@@ -30,6 +30,7 @@
 UNROLL = GROUP
 SHARE = SIDE * SIDE // FRAMES
 DAMPING = 0.02 * FRAMES
+FAR_FIRST = (4, 3, 5, 2, 6, 1, 7)
 MESH = pl.DeviceIdType.MESH
 f32, bf16 = jnp.float32, jnp.bfloat16
 
@@ -69,21 +70,23 @@
         return cut(t)
 
     def twice(c, s):
-        high, low = columns_of(c, s)
-        return np.concatenate([high, np.zeros((128 - BOX, 256), high.dtype), high]), low
+        t = np.zeros((BOX, 256))
+        t[: c.shape[0], : c.shape[1]], t[: c.shape[0], 128 : 128 + c.shape[1]] = c, s
+        high, low = cut(t)
+        return np.concatenate([high, high, low])
 
     parts = {}
     c, s = pair(k, u)
     parts["pupil_rows"] = rows_of(c, s)
-    parts["pupil_columns"], parts["pupil_columns_low"] = twice(c.T, s.T)
-    parts["back_columns"], parts["back_columns_low"] = twice(weight[:, None] * c, weight[:, None] * s)
+    parts["pupil_columns"] = twice(c.T, s.T)
+    parts["back_columns"] = twice(weight[:, None] * c, weight[:, None] * s)
 
     def wide(t):
         return np.pad(t, ((0, BOX - t.shape[0]), (0, BOX - t.shape[1])))
 
     parts["back_even"], parts["back_odd"] = rows_of(wide(c.T * weight)), rows_of(wide(s.T * weight))
     c, s = pair(k, k)
-    parts["focal_columns"], parts["focal_columns_low"] = twice(weight[:, None] * c, -weight[:, None] * s)
+    parts["focal_columns"] = twice(weight[:, None] * c, -weight[:, None] * s)
     parts["focal_even"], parts["focal_odd"] = rows_of(wide(c * weight)), rows_of(wide(s * weight))
     w = profile()
     c, s = pair(k, y)
@@ -179,7 +182,7 @@
 
     def from_right(x, name, half=None):
         h, r = split(x)
-        return mm(lanes(h, r)[:, : 128 + BOX], table(name, half)) + mm(h[:, :BOX], table(name + "_low", half))
+        return mm(lanes(h[:, :BOX], r[:, :BOX], h[:, :BOX]), table(name, half))
 
     loads = [
         pltpu.make_async_copy(coef.at[0], coef_v, local_sem.at[0]),
@@ -197,12 +200,12 @@
     def greet(device):
         pl.semaphore_signal(barrier, inc=1, device_id=device, device_id_type=MESH)
 
+    for d in FAR_FIRST:
+        greet(at(me, lax.rem(z + d, DEPTH)))
+    for t in [*peers, me]:
+        greet(at(t, z, beside))
     for t in peers:
         greet(at(t, z))
-    for d in range(1, DEPTH):
-        greet(at(me, lax.rem(z + d, DEPTH)))
-    for j in range(GROUP):
-        greet(at(j, z, beside))
 
     skyp[pl.ds(0, RIM), :] = jnp.zeros((RIM, 256), f32)
     skyp[pl.ds(512 + RIM, 120), :] = jnp.zeros((120, 256), f32)
@@ -213,8 +216,9 @@
     loads[2].wait()
     for half in range(2):
         strip_t = skyp[:, half * 128 : half * 128 + 128].T
-        edges[2 * half] = strip_t[:8]
-        edges[2 * half + 1] = strip_t[120:]
+        for r in range(4):
+            edges[2 * half, r] = strip_t[:8, r * TILE : r * TILE + SIDE]
+            edges[2 * half + 1, r] = strip_t[120:, r * TILE : r * TILE + SIDE]
     pl.semaphore_wait(barrier, GROUP - 1 + DEPTH - 1 + GROUP)
 
     sends = []
@@ -233,7 +237,7 @@
         ]
 
     def edge_of(kind, t):
-        return edges.at[kind, :, pl.ds(pl.multiple_of(lax.rem(t, 4) * TILE, TILE), 256)]
+        return edges.at[kind, lax.rem(t, 4)]
 
     for t in peers:
         kind, side = jnp.where(t < 4, 2, 1), jnp.where(t < 4, 1, 0)
@@ -313,7 +317,7 @@
         pim[at_g, :] = m * sine
         return carry
 
-    lax.fori_loop(0, BOX // 8, pupils, 0, unroll=2)
+    lax.fori_loop(0, BOX // 8, pupils, 0, unroll=5)
 
     def of_frame(ref, f):
         return ref[pl.ds(f, BOX, stride=GROUP), :]
@@ -364,7 +368,8 @@
     row = lax.broadcasted_iota(jnp.int32, (128, 256), 0)
     left_on = jnp.where(jnp.logical_and(strip == 0, me < 4), 0.0, 1.0)
     right_on = jnp.where(jnp.logical_and(strip == STRIPS - 1, me >= 4), 0.0, 1.0)
-    rims = halo[...].reshape(128, 256) * jnp.where(lax.rem(row, 16) < 8, left_on, right_on)
+    rims = lanes(halo[...].reshape(128, SIDE), jnp.zeros((128, 256 - SIDE), f32))
+    rims = rims * jnp.where(lax.rem(row, 16) < 8, left_on, right_on)
     rims = rims.T[:SIDE]
     for f in range(GROUP):
         turned[f] = pltpu.roll(rims, (128 - 16 * f) % 128, 1) if f else rims
@@ -395,8 +400,10 @@
 
     arrive(close)
     data([me, *close])
-    arrive(distant)
-    data(distant)
+    arrive(distant[:2])
+    data(distant[:2])
+    arrive(distant[2:])
+    data(distant[2:])
 
     lane80 = lax.broadcasted_iota(jnp.int32, (BOX, 128), 1)
     lane40 = lax.broadcasted_iota(jnp.int32, (REST_ROWS, 128), 1)
@@ -415,7 +422,7 @@
                 part * BOX + d * CHUNK : part * BOX + (d + 1) * CHUNK, :
             ]
         sum_send[d, 3 * CHUNK :, :] = packed[3 * BOX + d * REST_CHUNK : 3 * BOX + (d + 1) * REST_CHUNK, :]
-    for d in range(1, DEPTH):
+    for d in FAR_FIRST:
         t = lax.rem(z + d, DEPTH)
         c = remote(sum_send.at[t], sum_recv.at[z], sum_ss.at[t], sum_rs.at[z], at(me, t))
         c.start()
@@ -436,7 +443,7 @@
     power = jnp.where(lane5 < 2 * REST, pltpu.roll(rest, 128 - 4 * REST, 1), pltpu.roll(rest, 128 - 2 * REST, 1))
     power = jnp.where(lane5 < 4 * REST, power, 0.0) + DAMPING
     obj_send[2 * CHUNK :, :] = rest / power
-    for d in range(1, DEPTH):
+    for d in FAR_FIRST:
         t = lax.rem(z + d, DEPTH)
         c = remote(obj_send, obj_all.at[z], obj_ss.at[t], obj_rs.at[z], at(me, t))
         c.start()
@@ -607,7 +614,7 @@
         vmem(TABLE.shape, bf16), vmem((640, 256), f32), vmem((GROUP, MODES), f32),
         vmem((64, 128), f32), vmem((64, 128), f32), vmem((SIDE, SIDE), jnp.int32), vmem((MODES, FLAT), f32),
         vmem((3 * MODES, FLAT), bf16),
-        vmem((4, 8, 640), f32), vmem((GROUP, SIDE, 128), f32), vmem((GROUP, 2, 8, 256), f32),
+        vmem((4, 4, 8, SIDE), f32), vmem((GROUP, SIDE, 128), f32), vmem((GROUP, 2, 8, SIDE), f32),
         vmem((GROUP, SIDE, 128), f32), vmem((8 * BOX, 128), f32), vmem((8 * BOX, 128), f32),
         *[vmem((GROUP, 2 * BOX, 128), f32)] * 8,
         vmem((3, 2 * BOX, 128), f32), vmem((3 * BOX + REST_ROWS, 128), f32),

time: 46.5 us -> 44.1 us (0.948)
  Pallas kernels: 44.6 us -> 42.1 us
    pallas_call x1, Pallas kernels: 44.6 us -> 42.1 us  [body(): pl.pallas_call(kernel, out_shape=(pltpu.VMEM((1, GROUP, MODES), f32), plt...]
where the time goes in v5:
time: 44.1 us; the launch traced here: 43.9 us
  Pallas kernels  42.1 us (95%)
  local copies, waits for them, and re-layouts  1.2 us (3%)
  between operations  0.64 us (1%)
    pallas_call x1, Pallas kernels, body(): pl.pallas_call(kernel, out_shape=(pltpu.VMEM((1, GROUP, MODES), f32), plt...  42.1 us
    unnamed x2, local copies, waits for them, and re-layouts  1.2 us

profile of v5, /device:TPU:4, one launch (start us, length us, event | category | flops | bytes accessed | tf_op | source)
XLA Modules:
  0.0 43.9 jit_solution(17393248179479962070)
XLA Ops:
  0.6 42.1 %shard_map.68 = (f32[1,8,64]{2,1,0:T(8,128)S(1)}, f32[8,2,324]{2,1,0:T(2,128)S(1)}) custom-call(f32[1,512,256]{2,1,0:T(8,128)} %sky.1, f32[1,8,64]{2,1,0:T(8,128)} %coef.1, f32[64,20736]{1,0:T(8,128)} %basis.1, s32[144,144]{1,0:T(8,128)} %aperture.1, bf16[1808,256]{1,0:T(8,128)(2,1)} %constant.2.clone.table_hbm), custom_call_target="tpu_custom_call" | custom-call | tf_op jit(solution)/shard_map/pallas_call | solution.py:627
  42.7 0.6 %copy.9 = f32[1,8,64]{2,1,0:T(8,128)} copy(f32[1,8,64]{2,1,0:T(8,128)S(1)} %get-tuple-element.2) | data formatting | bytes 4096
  43.3 0.6 %copy.10 = f32[8,2,324]{2,1,0:T(2,128)} copy(f32[8,2,324]{2,1,0:T(2,128)S(1)} %get-tuple-element.3) | data formatting | bytes 41472

commit v6 on v5

--- a/solution.py
+++ b/solution.py
@@ -18,12 +18,8 @@
 STRIPS = 4
 FRAMES = GROUP * DEPTH
 HALF = SIDE // 2 + 1
-CHUNK = BOX // DEPTH
-MAIN, REST = 64, HALF - 64
-REST_ROWS = 40
-REST_CHUNK = REST_ROWS // DEPTH
-SUMS = 3 * CHUNK + REST_CHUNK
-OBJECTS = 2 * CHUNK + REST_CHUNK
+FOLD = BOX // 2
+CHUNK = FOLD // DEPTH
 FLAT = BOX * SIDE
 PERIOD = 8 * SIDE
 MODES = 64
@@ -87,10 +83,15 @@
     parts["back_even"], parts["back_odd"] = rows_of(wide(c.T * weight)), rows_of(wide(s.T * weight))
     c, s = pair(k, k)
     parts["focal_columns"] = twice(weight[:, None] * c, -weight[:, None] * s)
-    parts["focal_even"], parts["focal_odd"] = rows_of(wide(c * weight)), rows_of(wide(s * weight))
+    disc = np.concatenate([np.arange(37), [0] * 3, np.arange(72, 36, -1), [0] * 4])
+    used = np.concatenate([np.ones(37), [0] * 3, np.ones(36), [0] * 4])
+    parts["focal_even"] = rows_of(wide((c * weight)[disc] * used[:, None]))
+    parts["focal_odd"] = rows_of(wide((s * weight)[disc] * used[:, None]))
+    parts["disc_even"] = rows_of(wide((c * weight)[:, disc] * used))
+    parts["disc_odd"] = rows_of(wide((s * weight)[:, disc] * used))
     w = profile()
     c, s = pair(k, y)
-    t = rows_of(c * w / SIDE, s * w / SIDE)
+    t = rows_of((c * w / SIDE)[disc] * used[:, None], (s * w / SIDE)[disc] * used[:, None])
     parts["data_rows"], parts["data_rows_end"] = t[:, :256], t[:, 256:]
     order = np.concatenate([y[RIM:-RIM], y[:RIM], y[-RIM:]])
     parts["data_columns"], parts["data_columns_low"] = columns_of(
@@ -147,10 +148,10 @@
     gradient_out, object_out,
     tab, skyp, coef_v, coef_send, coef_recv, mask_v, base, base3,
     edges, img, halo, turned, pre, pim, fpr, fpi, fmr, fmi, tre, tim, dre, dim_,
-    sums, packed, sum_send, sum_recv, sum_v, obj_send, obj_all, ore, oim, dph,
+    sums, packed, pow_send, pow_recv, sum_send, sum_recv, obj_send, obj_all, ore, oim, dph,
     full, out_send, out_recv, part_send, part_recv, ret_send, ret_recv,
     local_sem, coef_ss, coef_rs, img_ss, img_rs, own_ss, own_rs, cross_ss, cross_rs,
-    sum_ss, sum_rs, obj_ss, obj_rs, out_ss, out_rs, ret_ss, ret_rs, part_sem,
+    pow_ss, pow_rs, sum_ss, sum_rs, obj_ss, obj_rs, out_ss, out_rs, ret_ss, ret_rs, part_sem,
 ):
     place, strip = lax.axis_index("frame"), lax.axis_index("patch")
     me, z = place // DEPTH, place % DEPTH
@@ -211,8 +212,8 @@
     skyp[pl.ds(512 + RIM, 120), :] = jnp.zeros((120, 256), f32)
     loads[0].wait()
     for p in range(GROUP):
-        row = jnp.broadcast_to(coef_v[p : p + 1, :], (8, MODES))
-        coef_send[p * 8 : p * 8 + 8, :] = lanes(row, row)
+        row = coef_v[p : p + 1, :]
+        coef_send[p] = lanes(row, row)
     loads[2].wait()
     for half in range(2):
         strip_t = skyp[:, half * 128 : half * 128 + 128].T
@@ -222,14 +223,11 @@
     pl.semaphore_wait(barrier, GROUP - 1 + DEPTH - 1 + GROUP)
 
     sends = []
-    def rows8(ref, j):
-        return ref.at[pl.ds(pl.multiple_of(j * 8, 8), 8)]
-
     for t in peers:
-        c = remote(rows8(coef_send, t), rows8(coef_recv, me), coef_ss.at[t], coef_rs.at[me], at(t, z))
-        c.start()
-        sends.append(c)
-    coef_recv[pl.ds(pl.multiple_of(me * 8, 8), 8), :] = coef_send[pl.ds(pl.multiple_of(me * 8, 8), 8), :]
+        c = remote(coef_send.at[t], coef_recv.at[me], coef_ss.at[t], coef_rs.at[me], at(t, z))
+        c.start()
+        sends.append(c)
+    coef_recv[me] = coef_send[me]
 
     def main_of(t):
         return skyp.at[
@@ -288,8 +286,8 @@
     dph[0:BOX, :] = mask
 
     for j in peers:
-        remote(rows8(coef_send, j), rows8(coef_recv, j), coef_ss.at[j], coef_rs.at[j], at(j, z)).wait_recv()
-    weights = coef_recv[pl.ds(0, GROUP, stride=8), :]
+        remote(coef_send.at[j], coef_recv.at[j], coef_ss.at[j], coef_rs.at[j], at(j, z)).wait_recv()
+    weights = jnp.concatenate([coef_recv[j] for j in range(GROUP)])
     w0 = weights.astype(bf16).astype(f32)
     w1 = (weights - w0).astype(bf16).astype(f32)
     w2 = weights - w0 - w1
@@ -359,6 +357,33 @@
 
     lax.fori_loop(0, GROUP // UNROLL, transfers, 0)
 
+    lane40 = lax.broadcasted_iota(jnp.int32, (FOLD, 128), 1)
+    row40 = lax.broadcasted_iota(jnp.int32, (FOLD, 128), 0)
+    border = jnp.where(row40 < 24, 73, jnp.where(row40 < 32, 68, 65))
+
+    def shifted(x, back):
+        return stack(*[
+            pltpu.roll(x[a:b], 128 - by if back else by, 1) for a, b, by in ((0, 24, 73), (24, 32, 68), (32, 40, 65))
+        ])
+
+    def pack(x, into, at_row):
+        for sign in range(2):
+            wide, narrow = x[sign * BOX : sign * BOX + FOLD], x[sign * BOX + FOLD : (sign + 1) * BOX]
+            packed[...] = jnp.where(lane40 < border, wide, shifted(narrow, False))
+            for d in range(DEPTH):
+                into[d, at_row + sign * CHUNK : at_row + (sign + 1) * CHUNK, :] = packed[d * CHUNK : (d + 1) * CHUNK, :]
+
+    power = jnp.zeros((2 * BOX, 128), f32)
+    for f in range(GROUP):
+        power = power + (tre[f] * tre[f] + tim[f] * tim[f])
+    pack(power, pow_send, 0)
+    for d in FAR_FIRST:
+        t = lax.rem(z + d, DEPTH)
+        c = remote(pow_send.at[t], pow_recv.at[z], pow_ss.at[t], pow_rs.at[z], at(me, t))
+        c.start()
+        sends.append(c)
+    pow_recv[z] = pow_send[z]
+
     for c in mine:
         c.wait()
     for j in range(GROUP):
@@ -379,7 +404,7 @@
     def data(fs):
         h, r = split(stack(*[lanes(img[f], turned[f]) for f in fs]))
         x = mm3((h[:, :SIDE], r[:, :SIDE]), (table("data_columns"), table("data_columns_low")))
-        n_re, n_im, power = sums[0], sums[1], sums[2]
+        n_re, n_im = sums[0], sums[1]
         for m, f in enumerate(fs):
             h, r = split(x[m * SIDE : (m + 1) * SIDE])
             h = stack(h, r, h)
@@ -391,8 +416,7 @@
             t_re, t_im = tre[f], tim[f]
             n_re = n_re + (t_re * d_re + t_im * d_im)
             n_im = n_im + (t_re * d_im - t_im * d_re)
-            power = power + (t_re * t_re + t_im * t_im)
-        sums[0], sums[1], sums[2] = n_re, n_im, power
+        sums[0], sums[1] = n_re, n_im
 
     def arrive(js):
         for j in js:
@@ -405,44 +429,28 @@
     arrive(distant[2:])
     data(distant[2:])
 
-    lane80 = lax.broadcasted_iota(jnp.int32, (BOX, 128), 1)
-    lane40 = lax.broadcasted_iota(jnp.int32, (REST_ROWS, 128), 1)
-    rest = jnp.zeros((REST_ROWS, 128), f32)
-    for part in range(3):
-        plus, minus = sums[part, :BOX], sums[part, BOX:]
-        packed[part * BOX : (part + 1) * BOX, :] = jnp.where(lane80 < MAIN, plus, pltpu.roll(minus, MAIN, 1))
-        for sign, x in enumerate((plus, minus)):
-            j = (2 * part + sign) * REST
-            x = pltpu.roll(x[:REST_ROWS], (j - MAIN) % 128, 1)
-            rest = jnp.where(jnp.logical_and(lane40 >= j, lane40 < j + REST), x, rest)
-    packed[3 * BOX :, :] = rest
-    for d in range(DEPTH):
-        for part in range(3):
-            sum_send[d, part * CHUNK : (part + 1) * CHUNK, :] = packed[
-                part * BOX + d * CHUNK : part * BOX + (d + 1) * CHUNK, :
-            ]
-        sum_send[d, 3 * CHUNK :, :] = packed[3 * BOX + d * REST_CHUNK : 3 * BOX + (d + 1) * REST_CHUNK, :]
+    pack(sums[0], sum_send, 0)
+    pack(sums[1], sum_send, 2 * CHUNK)
     for d in FAR_FIRST:
         t = lax.rem(z + d, DEPTH)
         c = remote(sum_send.at[t], sum_recv.at[z], sum_ss.at[t], sum_rs.at[z], at(me, t))
         c.start()
         sends.append(c)
     sum_recv[z] = sum_send[z]
+    for d in range(1, DEPTH):
+        j = lax.rem(z + DEPTH - d, DEPTH)
+        remote(pow_send.at[j], pow_recv.at[j], pow_ss.at[j], pow_rs.at[j], at(me, j)).wait_recv()
+    power = pow_recv[0]
+    for j in range(1, DEPTH):
+        power = power + pow_recv[j]
+    power = power + DAMPING
     for d in range(1, DEPTH):
         j = lax.rem(z + DEPTH - d, DEPTH)
         remote(sum_send.at[j], sum_recv.at[j], sum_ss.at[j], sum_rs.at[j], at(me, j)).wait_recv()
     total = sum_recv[0]
     for j in range(1, DEPTH):
         total = total + sum_recv[j]
-    sum_v[...] = total
-    power = sum_v[2 * CHUNK : 3 * CHUNK, :] + DAMPING
-    obj_send[0:CHUNK, :] = sum_v[0:CHUNK, :] / power
-    obj_send[CHUNK : 2 * CHUNK, :] = sum_v[CHUNK : 2 * CHUNK, :] / power
-    rest = sum_v[3 * CHUNK :, :]
-    lane5 = lax.broadcasted_iota(jnp.int32, (REST_CHUNK, 128), 1)
-    power = jnp.where(lane5 < 2 * REST, pltpu.roll(rest, 128 - 4 * REST, 1), pltpu.roll(rest, 128 - 2 * REST, 1))
-    power = jnp.where(lane5 < 4 * REST, power, 0.0) + DAMPING
-    obj_send[2 * CHUNK :, :] = rest / power
+    obj_send[...] = total / stack(power, power)
     for d in FAR_FIRST:
         t = lax.rem(z + d, DEPTH)
         c = remote(obj_send, obj_all.at[z], obj_ss.at[t], obj_rs.at[z], at(me, t))
@@ -452,22 +460,14 @@
     for d in range(1, DEPTH):
         j = lax.rem(z + DEPTH - d, DEPTH)
         remote(obj_send, obj_all.at[j], obj_ss.at[j], obj_rs.at[j], at(me, j)).wait_recv()
-    for d in range(DEPTH):
-        for part in range(2):
-            packed[part * BOX + d * CHUNK : part * BOX + (d + 1) * CHUNK, :] = obj_all[
-                d, part * CHUNK : (part + 1) * CHUNK, :
-            ]
-        packed[3 * BOX + d * REST_CHUNK : 3 * BOX + (d + 1) * REST_CHUNK, :] = obj_all[d, 2 * CHUNK :, :]
-    rest = packed[3 * BOX :, :]
     for part, ref in enumerate((ore, oim)):
-        main = packed[part * BOX : (part + 1) * BOX, :]
         for sign in range(2):
-            j = (2 * part + sign) * REST
-            x = stack(pltpu.roll(rest, (MAIN - j) % 128, 1), jnp.zeros((BOX - REST_ROWS, 128), f32))
-            x = jnp.where(lane80 < HALF, x, 0.0)
-            ref[sign * BOX : (sign + 1) * BOX, :] = jnp.where(
-                lane80 < MAIN, pltpu.roll(main, MAIN, 1) if sign else main, x
-            )
+            at_row = (2 * part + sign) * CHUNK
+            for d in range(DEPTH):
+                packed[d * CHUNK : (d + 1) * CHUNK, :] = obj_all[d, at_row : at_row + CHUNK, :]
+            x = packed[...]
+            ref[sign * BOX : sign * BOX + FOLD, :] = jnp.where(lane40 < jnp.minimum(border, HALF), x, 0.0)
+            ref[sign * BOX + FOLD : (sign + 1) * BOX, :] = jnp.where(lane40 < 128 - border, shifted(x, True), 0.0)
 
     scale = 2.0 / (SIDE * SIDE)
 
@@ -481,8 +481,8 @@
             e_im = dim_[f] - (o_re * t_im + o_im * t_re)
             re_even, re_odd = fold(-scale * (e_re * o_re + e_im * o_im))
             im_even, im_odd = fold(scale * (e_re * o_im - e_im * o_re))
-            c = from_left("focal_even", lanes(re_even, im_even))
-            s = from_left("focal_odd", lanes(re_odd, im_odd))
+            c = from_left("disc_even", lanes(re_even, im_even))
+            s = from_left("disc_odd", lanes(re_odd, im_odd))
             cr, ci, sr, si = c[:, :128], c[:, 128:], s[:, :128], s[:, 128:]
             h_re += [cr - si, cr + si]
             h_im += [ci + sr, ci - sr]
@@ -548,7 +548,8 @@
     mirrored = r_at >= SIDE
     k = jnp.where(mirrored, r_at - SIDE, r_at)
     minus = (k >= HALF) != mirrored
-    k = jnp.where(k >= HALF, SIDE - k, k) + jnp.where(minus, BOX, 0)
+    k = jnp.where(k >= HALF, SIDE - k, k)
+    k = jnp.where(k > 36, FOLD + 72 - k, k) + jnp.where(minus, BOX, 0)
     pick_rows = jnp.where(k == c_at, 1.0, 0.0).astype(bf16)
     r_at = lax.broadcasted_iota(jnp.int32, (128, 256), 0)
     c_at = lax.broadcasted_iota(jnp.int32, (128, 256), 1)
@@ -612,17 +613,17 @@
     vmem, dma = pltpu.VMEM, pltpu.SemaphoreType.DMA
     scratch = [
         vmem(TABLE.shape, bf16), vmem((640, 256), f32), vmem((GROUP, MODES), f32),
-        vmem((64, 128), f32), vmem((64, 128), f32), vmem((SIDE, SIDE), jnp.int32), vmem((MODES, FLAT), f32),
+        vmem((GROUP, 1, 128), f32), vmem((GROUP, 1, 128), f32), vmem((SIDE, SIDE), jnp.int32), vmem((MODES, FLAT), f32),
         vmem((3 * MODES, FLAT), bf16),
         vmem((4, 4, 8, SIDE), f32), vmem((GROUP, SIDE, 128), f32), vmem((GROUP, 2, 8, SIDE), f32),
         vmem((GROUP, SIDE, 128), f32), vmem((8 * BOX, 128), f32), vmem((8 * BOX, 128), f32),
         *[vmem((GROUP, 2 * BOX, 128), f32)] * 8,
-        vmem((3, 2 * BOX, 128), f32), vmem((3 * BOX + REST_ROWS, 128), f32),
-        vmem((DEPTH, SUMS, 128), f32), vmem((DEPTH, SUMS, 128), f32), vmem((SUMS, 128), f32),
-        vmem((OBJECTS, 128), f32), vmem((DEPTH, OBJECTS, 128), f32), vmem((2 * BOX, 128), f32), vmem((2 * BOX, 128), f32),
+        vmem((2, 2 * BOX, 128), f32), vmem((FOLD, 128), f32),
+        *[vmem((DEPTH, 2 * CHUNK, 128), f32)] * 2, *[vmem((DEPTH, 4 * CHUNK, 128), f32)] * 2,
+        vmem((4 * CHUNK, 128), f32), vmem((DEPTH, 4 * CHUNK, 128), f32), vmem((2 * BOX, 128), f32), vmem((2 * BOX, 128), f32),
         vmem((8 * BOX, 128), f32), vmem((4, SIDE, 128), f32), vmem((GROUP, 8, 384), f32), vmem((GROUP, 8, 384), f32),
         vmem((1, 1, 128), f32), vmem((FRAMES, 1, 128), f32), vmem((GROUP, 1, 128), f32), vmem((GROUP, 1, 128), f32),
-        *[dma((8,))] * 17, dma((2,)),
+        *[dma((8,))] * 19, dma((2,)),
     ]
     return pl.pallas_call(
         kernel,

time: 44.1 us -> 43.2 us (0.980)
  Pallas kernels: 42.1 us -> 41.2 us
    pallas_call x1, Pallas kernels: 42.1 us -> 41.2 us  [body(): pl.pallas_call(kernel, out_shape=(pltpu.VMEM((1, GROUP, MODES), f32), plt...]
where the time goes in v6:
time: 43.2 us; the launch traced here: 43 us
  Pallas kernels  41.2 us (95%)
  local copies, waits for them, and re-layouts  1.2 us (3%)
  between operations  0.64 us (1%)
    pallas_call x1, Pallas kernels, body(): pl.pallas_call(kernel, out_shape=(pltpu.VMEM((1, GROUP, MODES), f32), plt...  41.2 us
    unnamed x2, local copies, waits for them, and re-layouts  1.2 us

profile of v6, /device:TPU:4, one launch (start us, length us, event | category | flops | bytes accessed | tf_op | source)
XLA Modules:
  0.0 43.0 jit_solution(8425660227389337243)
XLA Ops:
  0.6 41.2 %shard_map.68 = (f32[1,8,64]{2,1,0:T(8,128)S(1)}, f32[8,2,324]{2,1,0:T(2,128)S(1)}) custom-call(f32[1,512,256]{2,1,0:T(8,128)} %sky.1, f32[1,8,64]{2,1,0:T(8,128)} %coef.1, f32[64,20736]{1,0:T(8,128)} %basis.1, s32[144,144]{1,0:T(8,128)} %aperture.1, bf16[1968,256]{1,0:T(8,128)(2,1)} %constant.2.clone.table_hbm), custom_call_target="tpu_custom_call" | custom-call | tf_op jit(solution)/shard_map/pallas_call | solution.py:628
  41.8 0.6 %copy.9 = f32[1,8,64]{2,1,0:T(8,128)} copy(f32[1,8,64]{2,1,0:T(8,128)S(1)} %get-tuple-element.2) | data formatting | bytes 4096
  42.4 0.6 %copy.10 = f32[8,2,324]{2,1,0:T(2,128)} copy(f32[8,2,324]{2,1,0:T(2,128)S(1)} %get-tuple-element.3) | data formatting | bytes 41472

commit v7 on v6

--- a/solution.py
+++ b/solution.py
@@ -26,6 +26,7 @@
 UNROLL = GROUP
 SHARE = SIDE * SIDE // FRAMES
 DAMPING = 0.02 * FRAMES
+EXCHANGES = ("coef", "own", "cross", "img_close", "img_mid", "img_last", "pow", "sum", "obj", "out", "ret", "part")
 FAR_FIRST = (4, 3, 5, 2, 6, 1, 7)
 MESH = pl.DeviceIdType.MESH
 f32, bf16 = jnp.float32, jnp.bfloat16
@@ -150,8 +151,7 @@
     edges, img, halo, turned, pre, pim, fpr, fpi, fmr, fmi, tre, tim, dre, dim_,
     sums, packed, pow_send, pow_recv, sum_send, sum_recv, obj_send, obj_all, ore, oim, dph,
     full, out_send, out_recv, part_send, part_recv, ret_send, ret_recv,
-    local_sem, coef_ss, coef_rs, img_ss, img_rs, own_ss, own_rs, cross_ss, cross_rs,
-    pow_ss, pow_rs, sum_ss, sum_rs, obj_ss, obj_rs, out_ss, out_rs, ret_ss, ret_rs, part_sem,
+    local_sem, send_sem, recv_sem,
 ):
     place, strip = lax.axis_index("frame"), lax.axis_index("patch")
     me, z = place // DEPTH, place % DEPTH
@@ -166,10 +166,15 @@
     def at(group, depth, which=None):
         return {"frame": group * DEPTH + depth, "patch": strip if which is None else which}
 
-    def remote(src, dst, send, recv, device):
+    def remote(src, dst, exchange, device):
+        at_sem = EXCHANGES.index(exchange)
         return pltpu.make_async_remote_copy(
-            src_ref=src, dst_ref=dst, send_sem=send, recv_sem=recv, device_id=device, device_id_type=MESH
+            src_ref=src, dst_ref=dst, send_sem=send_sem.at[at_sem], recv_sem=recv_sem.at[at_sem],
+            device_id=device, device_id_type=MESH,
         )
+
+    def everything(ref, exchange):
+        return remote(ref, ref, exchange, at(peers[0], z))
 
     def table(name, half=None):
         row, count, width = FIRST[name]
@@ -222,11 +227,8 @@
             edges[2 * half + 1, r] = strip_t[120:, r * TILE : r * TILE + SIDE]
     pl.semaphore_wait(barrier, GROUP - 1 + DEPTH - 1 + GROUP)
 
-    sends = []
     for t in peers:
-        c = remote(coef_send.at[t], coef_recv.at[me], coef_ss.at[t], coef_rs.at[me], at(t, z))
-        c.start()
-        sends.append(c)
+        remote(coef_send.at[t], coef_recv.at[me], "coef", at(t, z)).start()
     coef_recv[me] = coef_send[me]
 
     def main_of(t):
@@ -239,25 +241,18 @@
 
     for t in peers:
         kind, side = jnp.where(t < 4, 2, 1), jnp.where(t < 4, 1, 0)
-        c = remote(edge_of(kind, t), halo.at[me, side], own_ss.at[t], own_rs.at[me], at(t, z))
-        c.start()
-        sends.append(c)
+        remote(edge_of(kind, t), halo.at[me, side], "own", at(t, z)).start()
     for p in range(GROUP):
         kind, side, step = (3, 0, 1) if p < 4 else (0, 1, STRIPS - 1)
-        c = remote(
-            edge_of(kind, p), halo.at[me, side], cross_ss.at[p], cross_rs.at[me],
-            at(p, z, lax.rem(strip + step, STRIPS)),
-        )
-        c.start()
-        sends.append(c)
-    for t in close + distant:
-        c = remote(main_of(t), img.at[me], img_ss.at[t], img_rs.at[me], at(t, z))
-        c.start()
-        sends.append(c)
+        remote(edge_of(kind, p), halo.at[me, side], "cross", at(p, z, lax.rem(strip + step, STRIPS))).start()
+    batches = {"img_close": close, "img_mid": distant[:2], "img_last": distant[2:]}
+    for exchange, partners in batches.items():
+        for t in partners:
+            remote(main_of(t), img.at[me], exchange, at(t, z)).start()
     own_side = jnp.where(me < 4, 1, 0)
     mine = [
-        pltpu.make_async_copy(main_of(me), img.at[me], local_sem.at[6]),
-        pltpu.make_async_copy(edge_of(jnp.where(me < 4, 2, 1), me), halo.at[me, own_side], local_sem.at[7]),
+        pltpu.make_async_copy(main_of(me), img.at[me], local_sem.at[5]),
+        pltpu.make_async_copy(edge_of(jnp.where(me < 4, 2, 1), me), halo.at[me, own_side], local_sem.at[6]),
     ]
     for c in mine:
         c.start()
@@ -285,8 +280,7 @@
     intensity_scale = 1.0 / (SIDE * SIDE * area)
     dph[0:BOX, :] = mask
 
-    for j in peers:
-        remote(coef_send.at[j], coef_recv.at[j], coef_ss.at[j], coef_rs.at[j], at(j, z)).wait_recv()
+    everything(coef_recv.at[pl.ds(0, GROUP - 1)], "coef").wait_recv()
     weights = jnp.concatenate([coef_recv[j] for j in range(GROUP)])
     w0 = weights.astype(bf16).astype(f32)
     w1 = (weights - w0).astype(bf16).astype(f32)
@@ -379,17 +373,14 @@
     pack(power, pow_send, 0)
     for d in FAR_FIRST:
         t = lax.rem(z + d, DEPTH)
-        c = remote(pow_send.at[t], pow_recv.at[z], pow_ss.at[t], pow_rs.at[z], at(me, t))
-        c.start()
-        sends.append(c)
+        remote(pow_send.at[t], pow_recv.at[z], "pow", at(me, t)).start()
     pow_recv[z] = pow_send[z]
 
     for c in mine:
         c.wait()
-    for j in range(GROUP):
-        remote(edge_of(0, 0), halo.at[j, 1 - own_side], cross_ss.at[j], cross_rs.at[j], at(j, z, beside)).wait_recv()
-    for j in peers:
-        remote(edge_of(0, j), halo.at[j, own_side], own_ss.at[j], own_rs.at[j], at(j, z)).wait_recv()
+    all_own, all_cross = halo.at[pl.ds(0, GROUP - 1), 0], halo.at[:, 0]
+    everything(all_cross, "cross").wait_recv()
+    everything(all_own, "own").wait_recv()
     row = lax.broadcasted_iota(jnp.int32, (128, 256), 0)
     left_on = jnp.where(jnp.logical_and(strip == 0, me < 4), 0.0, 1.0)
     right_on = jnp.where(jnp.logical_and(strip == STRIPS - 1, me >= 4), 0.0, 1.0)
@@ -418,48 +409,34 @@
             n_im = n_im + (t_re * d_im - t_im * d_re)
         sums[0], sums[1] = n_re, n_im
 
-    def arrive(js):
-        for j in js:
-            remote(main_of(j), img.at[j], img_ss.at[j], img_rs.at[j], at(j, z)).wait_recv()
-
-    arrive(close)
+    everything(img.at[pl.ds(0, 3)], "img_close").wait_recv()
     data([me, *close])
-    arrive(distant[:2])
+    everything(img.at[pl.ds(0, 2)], "img_mid").wait_recv()
     data(distant[:2])
-    arrive(distant[2:])
+    everything(img.at[pl.ds(0, 2)], "img_last").wait_recv()
     data(distant[2:])
 
     pack(sums[0], sum_send, 0)
     pack(sums[1], sum_send, 2 * CHUNK)
     for d in FAR_FIRST:
         t = lax.rem(z + d, DEPTH)
-        c = remote(sum_send.at[t], sum_recv.at[z], sum_ss.at[t], sum_rs.at[z], at(me, t))
-        c.start()
-        sends.append(c)
+        remote(sum_send.at[t], sum_recv.at[z], "sum", at(me, t)).start()
     sum_recv[z] = sum_send[z]
-    for d in range(1, DEPTH):
-        j = lax.rem(z + DEPTH - d, DEPTH)
-        remote(pow_send.at[j], pow_recv.at[j], pow_ss.at[j], pow_rs.at[j], at(me, j)).wait_recv()
+    everything(pow_recv.at[pl.ds(0, DEPTH - 1)], "pow").wait_recv()
     power = pow_recv[0]
     for j in range(1, DEPTH):
         power = power + pow_recv[j]
     power = power + DAMPING
-    for d in range(1, DEPTH):
-        j = lax.rem(z + DEPTH - d, DEPTH)
-        remote(sum_send.at[j], sum_recv.at[j], sum_ss.at[j], sum_rs.at[j], at(me, j)).wait_recv()
+    everything(sum_recv.at[pl.ds(0, DEPTH - 1)], "sum").wait_recv()
     total = sum_recv[0]
     for j in range(1, DEPTH):
         total = total + sum_recv[j]
     obj_send[...] = total / stack(power, power)
     for d in FAR_FIRST:
         t = lax.rem(z + d, DEPTH)
-        c = remote(obj_send, obj_all.at[z], obj_ss.at[t], obj_rs.at[z], at(me, t))
-        c.start()
-        sends.append(c)
+        remote(obj_send, obj_all.at[z], "obj", at(me, t)).start()
     obj_all[z] = obj_send[...]
-    for d in range(1, DEPTH):
-        j = lax.rem(z + DEPTH - d, DEPTH)
-        remote(obj_send, obj_all.at[j], obj_ss.at[j], obj_rs.at[j], at(me, j)).wait_recv()
+    everything(obj_all.at[pl.ds(0, DEPTH - 1)], "obj").wait_recv()
     for part, ref in enumerate((ore, oim)):
         for sign in range(2):
             at_row = (2 * part + sign) * CHUNK
@@ -535,11 +512,9 @@
     depths = [(z, 0)] + [(lax.rem(z + d, DEPTH), min(d, DEPTH - d)) for d in range(1, DEPTH)]
     ways = [(a + b, group, depth) for group, a in groups for depth, b in depths if a + b]
     for _, group, depth in sorted(ways, key=lambda way: -way[0]):
-        remote(part_send, part_recv.at[pl.ds(place, 1)], part_sem.at[0], part_sem.at[1], at(group, depth)).start()
+        remote(part_send, part_recv.at[pl.ds(place, 1)], "part", at(group, depth)).start()
     for t in peers:
-        c = remote(ret_send.at[t], ret_recv.at[me], ret_ss.at[t], ret_rs.at[me], at(t, z))
-        c.start()
-        sends.append(c)
+        remote(ret_send.at[t], ret_recv.at[me], "ret", at(t, z)).start()
     part_recv[place] = part_send[0]
     ret_recv[me] = ret_send[me]
 
@@ -585,28 +560,35 @@
         for i in range(GROUP):
             out_send[i, n : n + 1, :] = picked[i : i + 1]
     for t in peers:
-        c = remote(out_send.at[t], out_recv.at[me], out_ss.at[t], out_rs.at[me], at(t, z))
-        c.start()
-        sends.append(c)
+        remote(out_send.at[t], out_recv.at[me], "out", at(t, z)).start()
     out_recv[me] = out_send[me]
 
-    for j in peers:
-        remote(out_send.at[j], out_recv.at[j], out_ss.at[j], out_rs.at[j], at(j, z)).wait_recv()
+    rest = {
+        "coef": coef_recv.at[pl.ds(0, GROUP - 1)],
+        "own": all_own,
+        "cross": all_cross,
+        "img_close": img.at[pl.ds(0, 3)],
+        "img_mid": img.at[pl.ds(0, 2)],
+        "img_last": img.at[pl.ds(0, 2)],
+        "pow": pow_recv.at[pl.ds(0, DEPTH - 1)],
+        "sum": sum_recv.at[pl.ds(0, DEPTH - 1)],
+        "obj": obj_all.at[pl.ds(0, DEPTH - 1)],
+        "out": out_recv.at[pl.ds(0, GROUP - 1)],
+        "ret": ret_recv.at[pl.ds(0, GROUP - 1)],
+        "part": part_recv.at[pl.ds(0, FRAMES - 1)],
+    }
+    for exchange, ref in rest.items():
+        everything(ref, exchange).wait_send()
+    everything(rest["out"], "out").wait_recv()
     for p in range(GROUP):
         object_out[p] = out_recv[p, 0:2, :SHARE]
-    for j in peers:
-        remote(ret_send.at[j], ret_recv.at[j], ret_ss.at[j], ret_rs.at[j], at(j, z)).wait_recv()
-    arrived = part_recv.at[pl.ds(0, FRAMES - 1)]
-    arrived = remote(arrived, arrived, part_sem.at[0], part_sem.at[1], at(peers[0], z))
-    arrived.wait_recv()
+    everything(rest["ret"], "ret").wait_recv()
+    everything(rest["part"], "part").wait_recv()
     for p in range(GROUP):
         mean = part_recv[p * DEPTH]
         for n in range(1, DEPTH):
             mean = mean + part_recv[p * DEPTH + n]
         gradient_out[0, p : p + 1, :] = (ret_recv[p] - mean * (1.0 / FRAMES))[:, :MODES]
-    arrived.wait_send()
-    for c in sends:
-        c.wait_send()
 
 
 def body(sky_image, coefficients, mode_basis, aperture):
@@ -623,7 +605,7 @@
         vmem((4 * CHUNK, 128), f32), vmem((DEPTH, 4 * CHUNK, 128), f32), vmem((2 * BOX, 128), f32), vmem((2 * BOX, 128), f32),
         vmem((8 * BOX, 128), f32), vmem((4, SIDE, 128), f32), vmem((GROUP, 8, 384), f32), vmem((GROUP, 8, 384), f32),
         vmem((1, 1, 128), f32), vmem((FRAMES, 1, 128), f32), vmem((GROUP, 1, 128), f32), vmem((GROUP, 1, 128), f32),
-        *[dma((8,))] * 19, dma((2,)),
+        dma((7,)), dma((len(EXCHANGES),)), dma((len(EXCHANGES),)),
     ]
     return pl.pallas_call(
         kernel,

time: 43.2 us -> 42 us (0.972)
  Pallas kernels: 41.2 us -> 40 us
    pallas_call x1, Pallas kernels: 41.2 us -> 40 us  [body(): pl.pallas_call(kernel, out_shape=(pltpu.VMEM((1, GROUP, MODES), f32), plt...]
where the time goes in v7:
time: 42 us; the launch traced here: 41.8 us
  Pallas kernels  40 us (95%)
  local copies, waits for them, and re-layouts  1.2 us (3%)
  between operations  0.64 us (2%)
    pallas_call x1, Pallas kernels, body(): pl.pallas_call(kernel, out_shape=(pltpu.VMEM((1, GROUP, MODES), f32), plt...  40 us
    unnamed x2, local copies, waits for them, and re-layouts  1.2 us

profile of v7, /device:TPU:4, one launch (start us, length us, event | category | flops | bytes accessed | tf_op | source)
XLA Modules:
  0.0 41.8 jit_solution(16576955546952990881)
XLA Ops:
  0.6 40.0 %shard_map.68 = (f32[1,8,64]{2,1,0:T(8,128)S(1)}, f32[8,2,324]{2,1,0:T(2,128)S(1)}) custom-call(f32[1,512,256]{2,1,0:T(8,128)} %sky.1, f32[1,8,64]{2,1,0:T(8,128)} %coef.1, f32[64,20736]{1,0:T(8,128)} %basis.1, s32[144,144]{1,0:T(8,128)} %aperture.1, bf16[1968,256]{1,0:T(8,128)(2,1)} %constant.2.clone.table_hbm), custom_call_target="tpu_custom_call" | custom-call | tf_op jit(solution)/shard_map/pallas_call | solution.py:610
  40.6 0.6 %copy.9 = f32[1,8,64]{2,1,0:T(8,128)} copy(f32[1,8,64]{2,1,0:T(8,128)S(1)} %get-tuple-element.2) | data formatting | bytes 4096
  41.2 0.6 %copy.10 = f32[8,2,324]{2,1,0:T(2,128)} copy(f32[8,2,324]{2,1,0:T(2,128)S(1)} %get-tuple-element.3) | data formatting | bytes 41472

commit v8 on v7

--- a/solution.py
+++ b/solution.py
@@ -276,9 +276,7 @@
     mask = mask_v[LOW : LOW + BOX, 0:128].astype(f32)
     mask = pltpu.roll(mask, 128 - LOW, 1)
     mask = jnp.where(lax.broadcasted_iota(jnp.int32, (BOX, 128), 1) < BOX, mask, 0.0)
-    area = jnp.sum(mask)
-    intensity_scale = 1.0 / (SIDE * SIDE * area)
-    dph[0:BOX, :] = mask
+    dph[0:BOX, :] = mask * jnp.sqrt(jnp.full((BOX, 128), 1.0 / (SIDE * SIDE), f32) / jnp.sum(mask))
 
     everything(coef_recv.at[pl.ds(0, GROUP - 1)], "coef").wait_recv()
     weights = jnp.concatenate([coef_recv[j] for j in range(GROUP)])
@@ -334,8 +332,8 @@
             p_re, p_im = r[:, :128] + i[:, 128:], i[:, :128] - r[:, 128:]
             m_re, m_im = r[:, :128] - i[:, 128:], i[:, :128] + r[:, 128:]
             fpr[f], fpi[f], fmr[f], fmi[f] = p_re, p_im, m_re, m_im
-            plus = (p_re * p_re + p_im * p_im) * intensity_scale
-            minus = (m_re * m_re + m_im * m_im) * intensity_scale
+            plus = p_re * p_re + p_im * p_im
+            minus = m_re * m_re + m_im * m_im
             even += fold(plus + minus)
             odd += fold(plus - minus)
         x_re = from_right(stack(*even), "focal_columns", 0)
@@ -446,25 +444,24 @@
             ref[sign * BOX : sign * BOX + FOLD, :] = jnp.where(lane40 < jnp.minimum(border, HALF), x, 0.0)
             ref[sign * BOX + FOLD : (sign + 1) * BOX, :] = jnp.where(lane40 < 128 - border, shifted(x, True), 0.0)
 
-    scale = 2.0 / (SIDE * SIDE)
+    scale = 4.0 * 2.0 / (SIDE * SIDE)
 
     def back(n, carry):
         fs = [n * UNROLL + m for m in range(UNROLL)]
-        o_re, o_im = ore[...], oim[...]
+        o_re, o_im = -scale * ore[...], -scale * oim[...]
+        o_square = scale * (ore[...] * ore[...] + oim[...] * oim[...])
         h_re, h_im = [], []
         for f in fs:
-            t_re, t_im = tre[f], tim[f]
-            e_re = dre[f] - (o_re * t_re - o_im * t_im)
-            e_im = dim_[f] - (o_re * t_im + o_im * t_re)
-            re_even, re_odd = fold(-scale * (e_re * o_re + e_im * o_im))
-            im_even, im_odd = fold(scale * (e_re * o_im - e_im * o_re))
+            d_re, d_im = dre[f], dim_[f]
+            re_even, re_odd = fold(d_re * o_re + d_im * o_im + o_square * tre[f])
+            im_even, im_odd = fold(d_im * o_re - d_re * o_im + o_square * tim[f])
             c = from_left("disc_even", lanes(re_even, im_even))
             s = from_left("disc_odd", lanes(re_odd, im_odd))
             cr, ci, sr, si = c[:, :128], c[:, 128:], s[:, :128], s[:, 128:]
             h_re += [cr - si, cr + si]
             h_im += [ci + sr, ci - sr]
-        even = from_right(stack(*h_re), "focal_columns", 0) * (4.0 * intensity_scale)
-        odd = from_right(stack(*h_im), "focal_columns", 1) * (4.0 * intensity_scale)
+        even = from_right(stack(*h_re), "focal_columns", 0)
+        odd = from_right(stack(*h_im), "focal_columns", 1)
         sum_rows, gap_rows = [], []
         for m, f in enumerate(fs):
             at_m = slice(2 * m * BOX, 2 * (m + 1) * BOX)

time: 42 us -> 41.9 us (level)
  no operation moved by 1% of the time
where the time goes in v8:
time: 41.9 us; the launch traced here: 41.8 us
  Pallas kernels  40 us (95%)
  local copies, waits for them, and re-layouts  1.2 us (3%)
  between operations  0.64 us (2%)
    pallas_call x1, Pallas kernels, body(): pl.pallas_call(kernel, out_shape=(pltpu.VMEM((1, GROUP, MODES), f32), plt...  40 us
    unnamed x2, local copies, waits for them, and re-layouts  1.2 us

profile of v8, /device:TPU:4, one launch (start us, length us, event | category | flops | bytes accessed | tf_op | source)
XLA Modules:
  0.0 41.8 jit_solution(1561876551805751750)
XLA Ops:
  0.6 40.0 %shard_map.68 = (f32[1,8,64]{2,1,0:T(8,128)S(1)}, f32[8,2,324]{2,1,0:T(2,128)S(1)}) custom-call(f32[1,512,256]{2,1,0:T(8,128)} %sky.1, f32[1,8,64]{2,1,0:T(8,128)} %coef.1, f32[64,20736]{1,0:T(8,128)} %basis.1, s32[144,144]{1,0:T(8,128)} %aperture.1, bf16[1968,256]{1,0:T(8,128)(2,1)} %constant.2.clone.table_hbm), custom_call_target="tpu_custom_call" | custom-call | tf_op jit(solution)/shard_map/pallas_call | solution.py:607
  40.6 0.6 %copy.9 = f32[1,8,64]{2,1,0:T(8,128)} copy(f32[1,8,64]{2,1,0:T(8,128)S(1)} %get-tuple-element.2) | data formatting | bytes 4096
  41.2 0.6 %copy.10 = f32[8,2,324]{2,1,0:T(2,128)} copy(f32[8,2,324]{2,1,0:T(2,128)S(1)} %get-tuple-element.3) | data formatting | bytes 41472

commit v9 on v8

--- a/solution.py
+++ b/solution.py
@@ -578,7 +578,7 @@
         everything(ref, exchange).wait_send()
     everything(rest["out"], "out").wait_recv()
     for p in range(GROUP):
-        object_out[p] = out_recv[p, 0:2, :SHARE]
+        object_out[p] = out_recv[p, :, :SHARE]
     everything(rest["ret"], "ret").wait_recv()
     everything(rest["part"], "part").wait_recv()
     for p in range(GROUP):
@@ -600,7 +600,7 @@
         vmem((2, 2 * BOX, 128), f32), vmem((FOLD, 128), f32),
         *[vmem((DEPTH, 2 * CHUNK, 128), f32)] * 2, *[vmem((DEPTH, 4 * CHUNK, 128), f32)] * 2,
         vmem((4 * CHUNK, 128), f32), vmem((DEPTH, 4 * CHUNK, 128), f32), vmem((2 * BOX, 128), f32), vmem((2 * BOX, 128), f32),
-        vmem((8 * BOX, 128), f32), vmem((4, SIDE, 128), f32), vmem((GROUP, 8, 384), f32), vmem((GROUP, 8, 384), f32),
+        vmem((8 * BOX, 128), f32), vmem((4, SIDE, 128), f32), vmem((GROUP, 2, 384), f32), vmem((GROUP, 2, 384), f32),
         vmem((1, 1, 128), f32), vmem((FRAMES, 1, 128), f32), vmem((GROUP, 1, 128), f32), vmem((GROUP, 1, 128), f32),
         dma((7,)), dma((len(EXCHANGES),)), dma((len(EXCHANGES),)),
     ]

time: 41.9 us -> 41.9 us (level)
  no operation moved by 1% of the time
where the time goes in v9:
time: 41.9 us; the launch traced here: 41.8 us
  Pallas kernels  40 us (95%)
  local copies, waits for them, and re-layouts  1.2 us (3%)
  between operations  0.64 us (2%)
    pallas_call x1, Pallas kernels, body(): pl.pallas_call(kernel, out_shape=(pltpu.VMEM((1, GROUP, MODES), f32), plt...  40 us
    unnamed x2, local copies, waits for them, and re-layouts  1.2 us

profile of v9, /device:TPU:4, one launch (start us, length us, event | category | flops | bytes accessed | tf_op | source)
XLA Modules:
  0.0 41.8 jit_solution(16446477052231349281)
XLA Ops:
  0.6 40.0 %shard_map.68 = (f32[1,8,64]{2,1,0:T(8,128)S(1)}, f32[8,2,324]{2,1,0:T(2,128)S(1)}) custom-call(f32[1,512,256]{2,1,0:T(8,128)} %sky.1, f32[1,8,64]{2,1,0:T(8,128)} %coef.1, f32[64,20736]{1,0:T(8,128)} %basis.1, s32[144,144]{1,0:T(8,128)} %aperture.1, bf16[1968,256]{1,0:T(8,128)(2,1)} %constant.2.clone.table_hbm), custom_call_target="tpu_custom_call" | custom-call | tf_op jit(solution)/shard_map/pallas_call | solution.py:607
  40.6 0.6 %copy.9 = f32[1,8,64]{2,1,0:T(8,128)} copy(f32[1,8,64]{2,1,0:T(8,128)S(1)} %get-tuple-element.2) | data formatting | bytes 4096
  41.2 0.6 %copy.10 = f32[8,2,324]{2,1,0:T(2,128)} copy(f32[8,2,324]{2,1,0:T(2,128)S(1)} %get-tuple-element.3) | data formatting | bytes 41472

commit v10 on v9

--- a/solution.py
+++ b/solution.py
@@ -501,8 +501,6 @@
     total = total[:8] + total[8:]
     gradient = total + pltpu.roll(total, MODES, 1)
 
-    for j in range(GROUP):
-        ret_send[j] = gradient[j : j + 1]
     part_send[0] = jnp.sum(gradient, axis=0, keepdims=True)
 
     groups = list(zip([*peers, me], (3, 2, 2, 2, 1, 1, 1, 0)))
@@ -510,6 +508,8 @@
     ways = [(a + b, group, depth) for group, a in groups for depth, b in depths if a + b]
     for _, group, depth in sorted(ways, key=lambda way: -way[0]):
         remote(part_send, part_recv.at[pl.ds(place, 1)], "part", at(group, depth)).start()
+    for j in range(GROUP):
+        ret_send[j] = gradient[j : j + 1]
     for t in peers:
         remote(ret_send.at[t], ret_recv.at[me], "ret", at(t, z)).start()
     part_recv[place] = part_send[0]

time: 41.9 us -> 41.9 us (level)
  no operation moved by 1% of the time
where the time goes in v10:
time: 41.9 us; the launch traced here: 41.8 us
  Pallas kernels  40 us (95%)
  local copies, waits for them, and re-layouts  1.2 us (3%)
  between operations  0.64 us (2%)
    pallas_call x1, Pallas kernels, body(): pl.pallas_call(kernel, out_shape=(pltpu.VMEM((1, GROUP, MODES), f32), plt...  40 us
    unnamed x2, local copies, waits for them, and re-layouts  1.2 us

profile of v10, /device:TPU:4, one launch (start us, length us, event | category | flops | bytes accessed | tf_op | source)
XLA Modules:
  0.0 41.8 jit_solution(11228269433099705986)
XLA Ops:
  0.6 40.0 %shard_map.68 = (f32[1,8,64]{2,1,0:T(8,128)S(1)}, f32[8,2,324]{2,1,0:T(2,128)S(1)}) custom-call(f32[1,512,256]{2,1,0:T(8,128)} %sky.1, f32[1,8,64]{2,1,0:T(8,128)} %coef.1, f32[64,20736]{1,0:T(8,128)} %basis.1, s32[144,144]{1,0:T(8,128)} %aperture.1, bf16[1968,256]{1,0:T(8,128)(2,1)} %constant.2.clone.table_hbm), custom_call_target="tpu_custom_call" | custom-call | tf_op jit(solution)/shard_map/pallas_call | solution.py:607
  40.6 0.6 %copy.9 = f32[1,8,64]{2,1,0:T(8,128)} copy(f32[1,8,64]{2,1,0:T(8,128)S(1)} %get-tuple-element.2) | data formatting | bytes 4096
  41.2 0.6 %copy.10 = f32[8,2,324]{2,1,0:T(2,128)} copy(f32[8,2,324]{2,1,0:T(2,128)S(1)} %get-tuple-element.3) | data formatting | bytes 41472
